TPU v7x, 256 devices: a whole 4x4x8 slice. The times are simulated.
256 devices in a mesh: dp: 16 (over z, core), mp: 16 (over y, x).
Axes of the slice: x: 4, y: 4, z: 8, core: 2. Of those that a mesh axis runs over, the one named last changes fastest.
Arguments:
- intermediate_signal: bfloat16 [16, 1024, 14336], P('mp', None, 'dp'), may hold values from -6 to 6
- frozen_down_weight: bfloat16 [14336, 4096], P('dp', 'mp'), may hold values from -0.046875 to 0.046875
- lowdim_entry_matrices: bfloat16 [16, 16, 14336, 64], P('mp', None, 'dp'), may hold values from -0.046875 to 0.046875
- lowdim_exit_matrices: bfloat16 [16, 16, 64, 4096], P('mp', 'dp'), may hold values from -0.75 to 0.75
- result_sensitivity: bfloat16 [16, 1024, 4096], P('mp', 'dp'), may hold values from -6 to 6
- token_client_choice: int32 [16, 1024], P('mp'), may hold values from 0 to 15, as said below
- matrix_bank_position: int32 [16, 16], P('mp'), may hold values from 0 to 15, as said below
- shard_active_entries: int32 [16, 16], P('mp'), may hold values from 32 to 64, as said below
Outputs:
- customized_projection_result: bfloat16 [16, 1024, 4096], P('mp', 'dp')
- entry_matrix_derivative: float32 [16, 16, 14336, 64], P('mp', None, 'dp')
- exit_matrix_derivative: float32 [16, 16, 64, 4096], P('mp', 'dp')
Inputs may be any that keep to these rules, and one draw needn't show every extreme that they name: `token_client_choice`: rows s * 64 to (s + 1) * 64 - 1 of a group belong to device s of dp. The owner of adapter u is matrix_bank_position[u]. Of one device's live rows at most 8 have adapters of one owner, and in every group one owner gets exactly 8 live rows from every device. `matrix_bank_position`: in each group a permutation of the slots. The live rows of a device are its first shard_active_entries rows; in each group some device has 64.
All inputs are finite; a program needn't handle non-finite values.
Results may differ from a plain program's by a relative error of at most 0.0065.
Values may be sent and summed in bfloat16 or wider, within the bound.
A program may use at most 128 MiB of HBM per device.

v0:
```python
import jax
import jax.numpy as jnp
from jax import lax
from jax.sharding import PartitionSpec as P


def route_tables(user_ids, slot_table, counts, tok_dev, capacity, adapters_per_device):
    dp_size = counts.shape[0]
    row_total = user_ids.shape[0]
    adapter_list = slot_table.shape[0]
    adapter_range = jnp.arange(adapter_list, dtype=jnp.int32)
    named = user_ids[:, None] == adapter_range[None, :]
    storage = jnp.sum(jnp.where(named, slot_table[None, :], 0), axis=1)
    row_ids = jnp.arange(row_total, dtype=jnp.int32)
    source_of = row_ids // tok_dev
    by_source = source_of[:, None] == jnp.arange(dp_size, dtype=jnp.int32)[None, :]
    row_limit = jnp.sum(jnp.where(by_source, counts[None, :], 0), axis=1)
    is_live = row_ids % tok_dev < row_limit
    owners = storage // adapters_per_device
    local_slot = storage % adapters_per_device
    owner_marks = (
        (owners[:, None] == jnp.arange(dp_size, dtype=jnp.int32)[None, :]) & is_live[:, None]
    ).astype(jnp.int32)
    per_source = owner_marks.reshape(dp_size, tok_dev, dp_size)
    earlier = jnp.cumsum(per_source, axis=1) - per_source
    row_rank = jnp.sum(earlier * per_source, axis=2)
    slot_hits = per_source[:, :, :, None] * (
        row_rank[:, :, None, None] == jnp.arange(capacity, dtype=jnp.int32)[None, None, None, :]
    ).astype(jnp.int32)
    filled = jnp.sum(slot_hits, axis=1)
    slot_row = (
        jnp.sum(slot_hits * jnp.arange(tok_dev, dtype=jnp.int32)[None, :, None, None], axis=1)
        + (1 - filled) * tok_dev
    )
    slot_adapter = jnp.sum(
        slot_hits * local_slot.reshape(dp_size, tok_dev)[:, :, None, None], axis=1
    )
    choose = ((storage[:, None] == adapter_range[None, :]) & is_live[:, None]).astype(jnp.float32)
    return (choose, slot_row, filled, slot_adapter)


def split_parts(values):
    upper = values.astype(jnp.bfloat16)
    lower = (values - upper.astype(jnp.float32)).astype(jnp.bfloat16)
    return (upper, lower)


def on_device(
    intermediate_signal,
    frozen_down_weight,
    lowdim_entry_matrices,
    lowdim_exit_matrices,
    result_sensitivity,
    token_client_choice,
    matrix_bank_position,
    shard_active_entries,
):
    my_index = lax.axis_index("dp")
    dp_size = lax.axis_size("dp")
    device_rows = intermediate_signal[0]
    row_total = device_rows.shape[0]
    tok_dev = row_total // dp_size
    capacity = tok_dev // 8
    adapters_per_device = lowdim_exit_matrices.shape[1]
    adapter_rank_width = lowdim_exit_matrices.shape[2]
    feature_count = lowdim_exit_matrices.shape[3]
    choose, slot_row, filled, slot_adapter = route_tables(
        token_client_choice[0],
        matrix_bank_position[0],
        shard_active_entries[0],
        tok_dev,
        capacity,
        adapters_per_device,
    )
    base_part = jnp.dot(
        device_rows,
        lax.all_gather(frozen_down_weight, "mp", axis=1, tiled=True),
        preferred_element_type=jnp.float32,
    )
    rank_everything = jnp.einsum(
        "xz,szu->xsu", device_rows, lowdim_entry_matrices[0], preferred_element_type=jnp.float32
    )
    rank_part = jnp.sum(rank_everything * choose[:, :, None], axis=1)
    base_own, rank_own = (
        lax.psum_scatter(base_part, "dp", scatter_dimension=0, tiled=True),
        lax.psum_scatter(rank_part, "dp", scatter_dimension=0, tiled=True),
    )
    my_slots = lax.dynamic_index_in_dim(slot_row, my_index, 0, keepdims=False)
    padded_rank = jnp.concatenate(
        [rank_own, jnp.zeros((1, adapter_rank_width), jnp.float32)], axis=0
    )
    padded_grad = jnp.concatenate(
        [result_sensitivity[0], jnp.zeros((1, feature_count), jnp.bfloat16)], axis=0
    )
    send_rank = padded_rank[my_slots]
    send_grad = padded_grad[my_slots].astype(jnp.float32)
    recv_rank, recv_grad = (
        lax.all_to_all(send_rank, "dp", split_axis=0, concat_axis=0, tiled=True),
        lax.all_to_all(send_grad, "dp", split_axis=0, concat_axis=0, tiled=True),
    )
    flat_rank = recv_rank.reshape(dp_size * capacity, adapter_rank_width)
    flat_grad = recv_grad.reshape(dp_size * capacity, feature_count).astype(jnp.bfloat16)
    mine_adapter = lax.dynamic_index_in_dim(slot_adapter, my_index, 1, keepdims=False).reshape(-1)
    mine_filled = lax.dynamic_index_in_dim(filled, my_index, 1, keepdims=False)
    marks = ((mine_adapter == 0) & (mine_filled.reshape(-1) > 0))[:, None]
    rank_upper, rank_lower = split_parts(flat_rank * marks.astype(jnp.float32))
    masked_grad = flat_grad * marks.astype(jnp.bfloat16)
    output_map_weight = lowdim_exit_matrices[0, 0]
    adapter_contribution = jnp.dot(
        rank_upper, output_map_weight, preferred_element_type=jnp.float32
    ) + jnp.dot(rank_lower, output_map_weight, preferred_element_type=jnp.float32)
    outer_dims = (((0,), (0,)), ((), ()))
    derivative_fragments = [
        lax.dot_general(rank_upper, flat_grad, outer_dims, preferred_element_type=jnp.float32)
        + lax.dot_general(rank_lower, flat_grad, outer_dims, preferred_element_type=jnp.float32)
    ]
    rank_back = lax.dot_general(
        masked_grad, output_map_weight, (((1,), (1,)), ((), ())), preferred_element_type=jnp.float32
    )
    exit_matrix_derivative = jnp.stack(derivative_fragments)[None]
    rank_grad = rank_back.reshape(dp_size, capacity, adapter_rank_width)
    returned = lax.all_to_all(
        adapter_contribution.reshape(dp_size, capacity, feature_count),
        "dp",
        split_axis=0,
        concat_axis=0,
        tiled=True,
    )
    placed = (
        jnp.zeros((tok_dev + 1, feature_count), jnp.float32)
        .at[my_slots.reshape(-1)]
        .add(returned.reshape(-1, feature_count))
    )
    total = base_own + placed[:tok_dev]
    customized_projection_result = total.astype(jnp.bfloat16)
    gathered = lax.all_gather(rank_grad[None], "dp", axis=0, tiled=True)
    owner_view = jnp.transpose(slot_row, (1, 0, 2))
    owner_filled = jnp.transpose(filled, (1, 0, 2))
    spots = jnp.where(
        owner_filled > 0,
        jnp.arange(dp_size, dtype=jnp.int32)[None, :, None] * tok_dev + owner_view,
        row_total,
    ).reshape(-1)
    rank_grad_rows = (
        jnp.zeros((row_total, adapter_rank_width), jnp.float32)
        .at[spots]
        .add(gathered.reshape(-1, adapter_rank_width), mode="drop")
    )
    grad_upper, grad_lower = split_parts(rank_grad_rows)
    choose_marks = choose.astype(jnp.bfloat16)[:, :, None]
    entry_matrix_derivative = jnp.einsum(
        "vg,vqh->qgh",
        device_rows,
        choose_marks * grad_upper[:, None, :],
        preferred_element_type=jnp.float32,
    )
    entry_matrix_derivative = entry_matrix_derivative + jnp.einsum(
        "vg,vqh->qgh",
        device_rows,
        choose_marks * grad_lower[:, None, :],
        preferred_element_type=jnp.float32,
    )
    return (
        customized_projection_result[None],
        entry_matrix_derivative[None],
        exit_matrix_derivative,
    )


def solution(mesh):
    in_specs = (
        P("mp", None, "dp"),
        P("dp", "mp"),
        P("mp", None, "dp", None),
        P("mp", "dp", None, None),
        P("mp", "dp", None),
        P("mp", None),
        P("mp", None),
        P("mp", None),
    )
    out_specs = (P("mp", "dp", None), P("mp", None, "dp", None), P("mp", "dp", None, None))
    return jax.shard_map(
        on_device, mesh=mesh, in_specs=in_specs, out_specs=out_specs, check_vma=False
    )
```

profile of v0, /device:TPU:1, one launch (start us, length us, event | category | flops | bytes accessed | tf_op | source)
XLA Modules:
  0.0 291.7 jit_solution(618486240489323896)
XLA Ops:
  11.0 3.9 %fusion.11 = f32[1024,1024]{0,1:S(1)} fusion(bf16[896,1024]{0,1:T(8,128)(2,1)} %bitcast.91, bf16[1,1024,896]{2,1,0:T(8,128)(2,1)S(1)} %copy-done), kind=kOutput, calls=%fused_computation.20 | convolution fusion | flops 1879048192 | bytes 7864320
  15.4 1.0 copy.67
  16.6 74.1 %all-gather.3.cloned.1.call-done = bf16[896,4096]{1,0:T(8,128)(2,1)} async-done(((bf16[896,256]{1,0:T(8,128)(2,1)}), bf16[896,4096]{1,0:T(8,128)(2,1)}) %all-gather.3.cloned.1.call-update) | async-done | bytes 7340048 | tf_op jit(solution)/shard_map/all_gather | solution.py:77
  90.8 14.3 %fusion.13 = f32[1024,4096]{1,0:T(8,128)} fusion(bf16[896,4096]{1,0:T(8,128)(2,1)} %all-gather.3.cloned.1.call-done, bf16[1,1024,896]{2,1,0:T(8,128)(2,1)S(1)} %copy-done), kind=kOutput, calls=%fused_computation.22 | convolution fusion | flops 7516192768 | bytes 25952256 | tf_op jit(solution)/shard_map/dot_general | solution.py:75
  105.4 1.7 select_reduce_fusion
  107.8 8.7 %multiply_reduce_fusion.1 = (s32[16,16,8]{2,1,0:T(8,128)S(1)}, s32[16,16,8]{2,1,0:T(8,128)S(1)}) fusion(s32[16,64,8]{1,2,0:T(8,128)S(1)} %fusion.43, s32[16,64,16]{1,2,0:T(8,128)S(1)} %copy.65), kind=kLoop, calls=%fused_computation.24 | loop fusion | flops 520192 | bytes 114688 | tf_op jit(solution)/shard_map/reduce_sum | solution.py:30
  119.7 9.1 %all-to-all-start = ((f32[16,1,512]{2,1,0:T(1,128)}), f32[16,1,512]{2,1,0:T(1,128)S(1)}, u32[]{:S(2)}, u32[]{:S(2)}) async-start(f32[16,1,512]{2,1,0:T(1,128)} %reshape.381), calls=%async_computation.2 | async-start | bytes 65536 | tf_op jit(solution)/shard_map/all_to_all | solution.py:98
  128.8 2.2 gather_fusion.1
  130.9 5.4 %all-to-all-done = f32[16,1,512]{2,1,0:T(1,128)S(1)} async-done(((f32[16,1,512]{2,1,0:T(1,128)}), f32[16,1,512]{2,1,0:T(1,128)S(1)}, u32[]{:S(2)}, u32[]{:S(2)}) %all-to-all-start) | async-done | bytes 32800 | tf_op jit(solution)/shard_map/all_to_all | solution.py:98
  136.9 3.9 %all-to-all-start.2 = ((bf16[16,8,4096]{2,1,0:T(8,128)(2,1)}), bf16[16,8,4096]{2,1,0:T(8,128)(2,1)S(1)}, u32[]{:S(2)}, u32[]{:S(2)}) async-start(bf16[16,8,4096]{2,1,0:T(8,128)(2,1)} %bitcast.84), calls=%async_computation.4 | async-start | bytes 2097152 | tf_op jit(solution)/shard_map/all_to_all | solution.py:99
  141.6 1.5 reduce
  143.6 1.8 fusion
  145.4 28.3 %all-to-all-done.2 = bf16[16,8,4096]{2,1,0:T(8,128)(2,1)S(1)} async-done(((bf16[16,8,4096]{2,1,0:T(8,128)(2,1)}), bf16[16,8,4096]{2,1,0:T(8,128)(2,1)S(1)}, u32[]{:S(2)}, u32[]{:S(2)}) %all-to-all-start.2) | async-done | bytes 1048608 | tf_op jit(solution)/shard_map/all_to_all | solution.py:99
  173.6 4.5 %all-to-all-start.1 = ((f32[16,8,4096]{2,1,0:T(8,128)}), f32[16,8,4096]{2,1,0:T(8,128)}, u32[]{:S(2)}, u32[]{:S(2)}) async-start(f32[16,8,4096]{2,1,0:T(8,128)} %fusion), calls=%async_computation.3 | async-start | bytes 4194304 | tf_op jit(solution)/shard_map/all_to_all | solution.py:122
  178.2 1.6 copy.72
  179.8 1.0 reshape.330
  181.4 75.7 %all-gather = f32[256,8,64]{2,1,0:T(8,128)} all-gather(f32[16,8,64]{2,1,0:T(8,128)S(1)} %fusion.25), channel_id=2, replica_groups=mesh['dp'=16,'mp'=16] {'dp'}, dimensions={0}, use_global_device_ids=true | all-gather | bytes 557056 | tf_op jit(solution)/shard_map/all_gather | solution.py:136
  257.1 11.0 %scatter_custom_fusion.1 = f32[1024,64]{1,0:T(8,128)S(1)} fusion(s32[2048]{0:T(1024)S(1)} %bitcast.87, f32[256,8,64]{2,1,0:T(8,128)} %all-gather, f32[]{:T(128)} %constant.81.clone.1), kind=kCustom, calls=%fused_computation.30 | custom fusion | flops 131072 | bytes 786436 | tf_op jit(solution)/shard_map/scatter-add | solution.py:147
  268.1 0.9 copy.74
  269.4 1.4 fusion.2
  270.9 2.3 fusion.5
  273.2 4.2 %add_bitcast_fusion = f32[1,16,896,64]{2,3,1,0:T(8,128)} fusion(f32[16,64,896]{2,1,0:T(8,128)S(1)} %fusion.5, bf16[1,1024,896]{2,1,0:T(8,128)(2,1)S(1)} %copy-done, bf16[1024,64]{0,1:T(8,128)(2,1)S(1)} %get-tuple-element.6, bf16[1024,16]{0,1:T(8,128)(2,1)S(1)} %copy-done.5), kind=kOutput, calls=%fused_computation.11 | convolution fusion | flops 1881014272 | bytes 9338880 | tf_op jit(solution)/shard_map/vg,vqh->qgh/dot_general | solution.py:151
  277.4 4.7 %scatter_custom_fusion = f32[65,4096]{1,0:T(8,128)S(1)} fusion(s32[128]{0:T(128)S(1)} %fusion.61, f32[16,8,4096]{2,1,0:T(8,128)} %all-to-all-done.1, f32[]{:T(128)} %constant.81.clone.1), kind=kCustom, calls=%fused_computation.12 | custom fusion | flops 524288 | bytes 3162116 | tf_op jit(solution)/shard_map/scatter-add | solution.py:132
  282.2 2.1 fusion.30
  (63 shorter events, 10.9 us)
Async XLA Ops:
  8.0 3.0 %copy-start = (bf16[1,1024,896]{2,1,0:T(8,128)(2,1)S(1)}, bf16[1,1024,896]{2,1,0:T(8,128)(2,1)}, u32[]{:S(2)}) copy-start(bf16[1,1024,896]{2,1,0:T(8,128)(2,1)} %param.8) | copy-start | bytes 5505028
  8.0 82.7 %all-gather.3.cloned.1.call-start = ((), (), s32[]{:S(2)}) async-start(), calls=%async_computation.5 | async-start | bytes 7798784 | tf_op jit(solution)/shard_map/all_gather | solution.py:77
  8.7 108.8 %reduce-scatter.5.cloned.1.call-start = ((), (), s32[]{:S(2)}) async-start(), calls=%async_computation.7 | async-start | bytes 557056 | tf_op jit(solution)/shard_map/reduce_scatter | solution.py:86
  16.4 265.8 %reduce-scatter.3.cloned.1.call-start = ((), (), s32[]{:S(2)}) async-start(), calls=%async_computation.6 | async-start | bytes 17825792 | tf_op jit(solution)/shard_map/reduce_scatter | solution.py:85
  105.0 23.7 %copy-start.3 = (bf16[1,64,4096]{2,1,0:T(8,128)(2,1)S(1)}, bf16[1,64,4096]{2,1,0:T(8,128)(2,1)}, u32[]{:S(2)}) copy-start(bf16[1,64,4096]{2,1,0:T(8,128)(2,1)} %param.12) | copy-start | bytes 1572868
  119.7 16.7 %all-to-all-start = ((f32[16,1,512]{2,1,0:T(1,128)}), f32[16,1,512]{2,1,0:T(1,128)S(1)}, u32[]{:S(2)}, u32[]{:S(2)}) async-start(f32[16,1,512]{2,1,0:T(1,128)} %reshape.381), calls=%async_computation.2 | async-start | bytes 65536 | tf_op jit(solution)/shard_map/all_to_all | solution.py:98
  130.9 12.2 %copy-start.1 = (bf16[1,1,64,4096]{3,2,1,0:T(8,128)(2,1)S(1)}, bf16[1,1,64,4096]{3,2,1,0:T(8,128)(2,1)}, u32[]{:S(2)}) copy-start(bf16[1,1,64,4096]{3,2,1,0:T(8,128)(2,1)} %param.11) | copy-start | bytes 1572868
  136.3 0.6 copy-start.4
  136.9 36.7 %all-to-all-start.2 = ((bf16[16,8,4096]{2,1,0:T(8,128)(2,1)}), bf16[16,8,4096]{2,1,0:T(8,128)(2,1)S(1)}, u32[]{:S(2)}, u32[]{:S(2)}) async-start(bf16[16,8,4096]{2,1,0:T(8,128)(2,1)} %bitcast.84), calls=%async_computation.4 | async-start | bytes 2097152 | tf_op jit(solution)/shard_map/all_to_all | solution.py:99
  173.6 103.8 %all-to-all-start.1 = ((f32[16,8,4096]{2,1,0:T(8,128)}), f32[16,8,4096]{2,1,0:T(8,128)}, u32[]{:S(2)}, u32[]{:S(2)}) async-start(f32[16,8,4096]{2,1,0:T(8,128)} %fusion), calls=%async_computation.3 | async-start | bytes 4194304 | tf_op jit(solution)/shard_map/all_to_all | solution.py:122
  269.4 1.4 copy-start.2
  269.4 1.4 copy-start.5
Sparse Core Ops, SparseCore 0:
  11.2 79.4 all-gather.2
Sparse Core Ops, SparseCore 1:
  16.5 59.3 reduce-scatter.4
  105.1 172.6 reduce-scatter.2
where the time goes:
time: 292 us
  waiting for transfers between devices  109 us (37%)
  blocking collectives  75.7 us (26%)
  other arithmetic  33.5 us (11%)
  matrix products  29.2 us (10%)
  starting transfers between devices  17.7 us (6%)
  between operations  15.7 us (5%)
  local copies, waits for them, and re-layouts  11.3 us (4%)
    all_gather x1, blocking collectives, on_device(): gathered = lax.all_gather(rank_grad[None], 'dp', axis=0, tiled=True)  75.7 us
    all_gather x1, waiting for transfers between devices, on_device(): lax.all_gather(frozen_down_weight, 'mp', axis=1, tiled=True)  74.1 us
    all_to_all x1, waiting for transfers between devices, on_device(): lax.all_to_all(send_grad, 'dp', split_axis=0, concat_axis=0, tiled=True)  28.3 us
    dot_general x1, matrix products, on_device(): jnp.dot(device_rows, lax.all_gather(frozen_down_weight, 'mp', axis=1, til...  14.3 us
    scatter-add x1, other arithmetic, on_device(): rank_grad_rows = jnp.zeros((row_total, adapter_rank_width), jnp.float32)....  11 us
    all_to_all x1, starting transfers between devices, on_device(): lax.all_to_all(send_rank, 'dp', split_axis=0, concat_axis=0, tiled=True)  9.05 us
    reduce_sum x1, other arithmetic, route_tables(): filled = jnp.sum(slot_hits, axis=1)  8.7 us
  transfers between devices with their start and end apart: 6, of which 3 were waited for; matrix products, arithmetic and copies ran while one was open for 24% of the time, Pallas kernels for 0%

commit v1 on v0

v1 whole, which is shorter than its diff:
```python
import jax
import jax.numpy as jnp
from jax import lax
from jax.experimental import pallas as pl
from jax.experimental.pallas import tpu as pltpu
from jax.sharding import PartitionSpec as P

F32 = jnp.float32
BF16 = jnp.bfloat16
MESH = pl.DeviceIdType.MESH
SIDE = 4
RING = 8
CORES = 2
UP, DOWN = 3, 4
ORDER = [
    (0, 0), (1, 0), (3, 0), (0, 1),
    (0, 3), (1, 1), (3, 1), (1, 3),
    (3, 3), (2, 0), (0, 2), (1, 2),
    (2, 1), (2, 3), (3, 2), (2, 2),
]
GROUPS = 4
LANES = 128


def route(user_ids, slot_table, counts, n_src, cap):
    adapters = slot_table.shape[0]
    rows = user_ids.shape[0]
    tok = rows // n_src
    ids = jnp.arange(adapters, dtype=jnp.int32)
    storage = jnp.sum(jnp.where(user_ids[:, None] == ids[None, :], slot_table[None, :], 0), axis=1)
    place = jnp.arange(tok, dtype=jnp.int32)
    live = place[None, :] < counts[:, None]
    owner = jnp.where(live, storage.reshape(n_src, tok), -1)
    earlier = (owner[:, :, None] == owner[:, None, :]) & (place[None, None, :] < place[None, :, None])
    rank = jnp.sum(earlier.astype(jnp.int32), axis=2)
    slot = jnp.where(live, owner * cap + rank, -1)
    return owner, rank, slot


def halved(part, offset):
    dx, dy = offset
    first, last = (dx, dy) if part == 0 else (dy, dx)
    return last == 2 or (last == 0 and first == 2)


def exchange(
    x_ref, w_ref, b_ref, ranks_ref, sens_ref, put_ref,
    out_ref, exit_ref, grads_ref,
    x_sib, w_all, b_sib, b_all, y_all, rank_in, rank_own, rank_sib, rank_rows, sens_in, grad_out, grad_in,
    part_out, part_in, last_out, last_in, grad_sum,
    ag_send, ag_recv, rs_send, rs_recv, pair_send, pair_recv, all_send, all_recv,
):
    n = RING * CORES
    dp = lax.axis_index("dp")
    mp = lax.axis_index("mp")
    z, c = dp // CORES, dp % CORES
    my_y, my_x = mp // SIDE, mp % SIDE
    sib = dp + 1 - 2 * c
    depth = w_ref.shape[0]
    half = depth // 2
    rows = x_ref.shape[0]
    chip_rows = rows // RING
    own_rows = chip_rows // CORES
    wide = LANES * (len(ORDER) // GROUPS)
    features = b_ref.shape[1]
    width = b_ref.shape[0]

    def at_x(sign):
        return my_y * SIDE + (my_x + SIDE + sign) % SIDE

    def at_y(sign):
        return ((my_y + SIDE + sign) % SIDE) * SIDE + my_x

    barrier = pltpu.get_barrier_semaphore()
    for k in range(1, n):
        pl.semaphore_signal(barrier, inc=1, device_id={"dp": (dp + k) % n}, device_id_type=MESH)
    for to in (at_x(1), at_x(-1), at_y(1), at_y(-1)):
        pl.semaphore_signal(barrier, inc=1, device_id={"mp": to}, device_id_type=MESH)
    pl.semaphore_wait(barrier, n - 1 + 4)

    sent = []

    def send(src, dst, send_sem, recv_sem, to):
        copy = pltpu.make_async_remote_copy(
            src_ref=src, dst_ref=dst, send_sem=send_sem, recv_sem=recv_sem, device_id=to, device_id_type=MESH
        )
        copy.start()
        sent.append(copy)

    def arrived(dst, sem):
        pltpu.make_async_copy(dst, dst, sem).wait()

    names = {}

    def sem_of(part, offset, piece):
        return names.setdefault((part, offset, piece), len(names))

    def place(part, offset, piece=None):
        spot = ORDER.index(offset)
        cols = pl.ds(LANES * (spot % GROUPS), LANES)
        if piece is None:
            return w_all.at[part, spot // GROUPS, :, cols]
        return w_all.at[part, spot // GROUPS, pl.ds(half * piece, half), cols]

    def pass_on(axis, sign, part, offset, piece=None, src=None):
        dx, dy = offset
        seen = ((dx - sign) % SIDE, dy) if axis == "x" else (dx, (dy - sign) % SIDE)
        to = at_x(sign) if axis == "x" else at_y(sign)
        if src is None:
            src = place(part, offset, piece)
        num = sem_of(part, seen, piece)
        send(src, place(part, seen, piece), ag_send.at[num], ag_recv.at[num], {"mp": to})

    def got(part, offset):
        for piece in (0, 1) if halved(part, offset) else (None,):
            arrived(place(part, offset, piece), ag_recv.at[sem_of(part, offset, piece)])

    def both(axis, part, offset, src=None):
        for sign in (1, -1):
            pass_on(axis, sign, part, offset, None, src)

    def relay(axis, part, offset):
        away = offset[0] if axis == "x" else offset[1]
        if away == 1:
            pass_on(axis, -1, part, offset, 0)
        else:
            pass_on(axis, 1, part, offset, 1)

    own_cols = w_ref.at[:, pl.ds(pl.multiple_of(LANES * c, LANES), LANES)]
    sib_cols = w_ref.at[:, pl.ds(pl.multiple_of(LANES * (1 - c), LANES), LANES)]
    send(sib_cols, place(1, (0, 0)), pair_send.at[0], pair_recv.at[0], {"dp": sib})
    both("x", 0, (0, 0), own_cols)
    both("y", 0, (0, 0), own_cols)

    def to_all(sem, src_of, dst):
        def body(k, _):
            to = (dp + k) % n
            pltpu.make_async_remote_copy(
                src_ref=src_of(to), dst_ref=dst.at[dp], send_sem=all_send.at[sem], recv_sem=all_recv.at[sem],
                device_id={"dp": to}, device_id_type=MESH,
            ).start()
            return 0
        lax.fori_loop(1, n, body, 0)

    def all_done(sem, dst, src):
        arrived(dst.at[pl.ds(0, n - 1)], all_recv.at[sem])

    to_all(0, lambda to: ranks_ref.at[to], rank_in)
    send(x_ref, x_sib, pair_send.at[1], pair_recv.at[1], {"dp": sib})
    send(b_ref, b_sib, pair_send.at[2], pair_recv.at[2], {"dp": sib})
    to_all(1, lambda to: sens_ref.at[to], sens_in)

    w_all[0, 0, :, 0:LANES] = own_cols[...]
    rank_in[dp] = ranks_ref[dp]
    sens_in[dp] = sens_ref[dp]
    arrived(place(1, (0, 0)), pair_recv.at[0])
    both("y", 1, (0, 0))
    both("x", 1, (0, 0))

    for d in ((1, 0), (3, 0)):
        got(0, d)
        both("y", 0, d)
        relay("x", 0, d)
        e = (d[1], d[0])
        got(1, e)
        both("x", 1, e)
        relay("y", 1, e)

    all_done(0, rank_in, ranks_ref)
    total = rank_in[0].astype(F32)
    for k in range(1, n):
        total = total + rank_in[k].astype(F32)
    rank_own[...] = total
    send(rank_own, rank_sib, pair_send.at[3], pair_recv.at[3], {"dp": sib})
    arrived(b_sib, pair_recv.at[2])
    for g in range(GROUPS):
        for j in range(GROUPS):
            dx, dy = ORDER[g * GROUPS + j]
            m = ((my_y + dy) % SIDE) * SIDE + (my_x + dx) % SIDE
            col = pl.ds(pl.multiple_of(m * CORES * LANES + c * LANES, LANES), LANES)
            b_all[g, 0:width, j * LANES : (j + 1) * LANES] = b_ref[:, col]
            b_all[g, width : 2 * width, j * LANES : (j + 1) * LANES] = b_sib[:, col]
    arrived(rank_sib, pair_recv.at[3])
    lane = lax.broadcasted_iota(jnp.int32, rank_own.shape, 1)
    mine, theirs = rank_own[...], rank_sib[...]
    low = jnp.concatenate(
        [jnp.where(lane < width, mine, 0.0), jnp.where(lane < width, 0.0, pltpu.roll(theirs, width, 1))], axis=0
    ).astype(BF16)
    high = jnp.concatenate(
        [jnp.where(lane < width, pltpu.roll(mine, width, 1), 0.0), jnp.where(lane < width, 0.0, theirs)], axis=0
    ).astype(BF16)
    mid = rows // 2
    rank_rows[0:mid] = jnp.dot(put_ref[0:mid], low, preferred_element_type=F32).astype(BF16)
    rank_rows[mid:rows] = jnp.dot(put_ref[mid:rows], high, preferred_element_type=F32).astype(BF16)

    for d in ((1, 0), (3, 0)):
        e = (d[1], d[0])
        got(1, d)
        relay("x", 1, d)
        got(0, e)
        relay("y", 0, e)
    arrived(x_sib, pair_recv.at[1])

    def product(g):
        tile = rows // 4

        @pl.loop(0, 4)
        def _(i):
            at = pl.ds(pl.multiple_of(i * tile, tile), tile)
            y_all[g, at] = (
                jnp.dot(x_ref[at], w_all[0, g], preferred_element_type=F32)
                + jnp.dot(x_sib[at], w_all[1, g], preferred_element_type=F32)
                + jnp.dot(rank_rows[at], b_all[g], preferred_element_type=F32)
            )

    def sem_rs(g, way, step):
        return g * (UP + DOWN) + (step - 1 if way > 0 else UP + step - 1)

    def hop(g, step):
        for way, length in ((-1, DOWN), (1, UP)):
            if step > length:
                continue
            dest = (z + RING + way * (length + 1 - step)) % RING
            value = y_all[g, pl.ds(pl.multiple_of(dest * chip_rows, chip_rows), chip_rows)]
            if step > 1:
                before = sem_rs(g, way, step - 1)
                arrived(part_in.at[before], rs_recv.at[before])
                value = value + part_in[before].astype(F32)
            num = sem_rs(g, way, step)
            part_out[num] = value.astype(BF16)
            to = ((z + RING + way) % RING) * CORES + c
            send(part_out.at[num], part_in.at[num], rs_send.at[num], rs_recv.at[num], {"dp": to})

    def store(value, g, core):
        for j in range(GROUPS):
            dx, dy = ORDER[g * GROUPS + j]
            m = ((my_y + dy) % SIDE) * SIDE + (my_x + dx) % SIDE
            col = pl.ds(pl.multiple_of(m * CORES * LANES + core * LANES, LANES), LANES)
            out_ref[:, col] = value[:, j * LANES : (j + 1) * LANES]

    def finish(g):
        up, down = sem_rs(g, 1, UP), sem_rs(g, -1, DOWN)
        arrived(part_in.at[up], rs_recv.at[up])
        arrived(part_in.at[down], rs_recv.at[down])

        def rows_of(core):
            part = pl.ds(pl.multiple_of(core * own_rows, own_rows), own_rows)
            base = y_all[g, pl.ds(pl.multiple_of(z * chip_rows + core * own_rows, own_rows), own_rows)]
            return (base + part_in[up, part].astype(F32) + part_in[down, part].astype(F32)).astype(BF16)

        last_out[g] = rows_of(1 - c)
        send(last_out.at[g], last_in.at[g], pair_send.at[4 + g], pair_recv.at[4 + g], {"dp": sib})
        store(rows_of(c), g, c)

    def close(g):
        arrived(last_in.at[g], pair_recv.at[4 + g])
        store(last_in[g], g, 1 - c)

    product(0)
    hop(0, 1)
    for d in ((1, 1), (3, 1)):
        got(1, d)
        relay("x", 1, d)
        e = (d[1], d[0])
        got(0, e)
        relay("y", 0, e)
    for d in ((1, 3), (3, 3)):
        got(1, d)
        relay("x", 1, d)
        e = (d[1], d[0])
        got(0, e)
        relay("y", 0, e)
    got(0, (2, 0))
    both("y", 0, (2, 0))
    got(1, (0, 2))
    both("x", 1, (0, 2))
    product(1)
    hop(1, 1)
    hop(0, 2)

    all_done(1, sens_in, sens_ref)
    mine = rank_own[...]
    ranks = jnp.concatenate([mine[:, 0:width], mine[:, width : 2 * width]], axis=0).astype(BF16)
    grad_sum[...] = jnp.zeros_like(grad_sum)

    @pl.loop(0, features // wide)
    def _(i):
        at = pl.ds(pl.multiple_of(i * wide, wide), wide)
        block = sens_in[:, :, at].astype(F32).reshape(ranks.shape[0], wide).astype(BF16)
        exit_ref[:, at] = lax.dot_general(ranks, block, (((0,), (0,)), ((), ())), preferred_element_type=F32)
        grad_sum[...] += lax.dot_general(block, b_ref[:, at], (((1,), (1,)), ((), ())), preferred_element_type=F32)

    grad = grad_sum[...]
    grad_out[...] = jnp.concatenate([grad[0 : grad.shape[0] // 2], grad[grad.shape[0] // 2 :]], axis=1).astype(BF16)
    to_all(2, lambda to: grad_out, grad_in)
    grad_in[dp] = grad_out[...]

    hop(1, 2)
    hop(0, 3)
    for d in ((1, 2), (3, 2)):
        got(1, d)
        relay("x", 1, d)
        e = (d[1], d[0])
        got(0, e)
        relay("y", 0, e)
    hop(1, 3)
    hop(0, 4)
    for part in (0, 1):
        for d in ((2, 0), (0, 2), (1, 2)):
            if (part, d) not in ((0, (2, 0)), (1, (0, 2)), (1, (1, 2))):
                got(part, d)
    product(2)
    hop(2, 1)
    hop(1, 4)
    finish(0)
    for part in (0, 1):
        for d in ((2, 1), (2, 3), (3, 2), (2, 2)):
            if (part, d) not in ((0, (2, 1)), (0, (2, 3)), (1, (3, 2))):
                got(part, d)
    hop(2, 2)
    product(3)
    hop(3, 1)
    finish(1)
    hop(2, 3)
    hop(3, 2)
    close(0)
    close(1)
    all_done(2, grad_in, grad_out)
    grads_ref[...] = grad_in[...]
    hop(2, 4)
    hop(3, 3)
    finish(2)
    hop(3, 4)
    finish(3)
    close(2)
    close(3)

    for copy in sent:
        copy.wait_send()
    for k, src in enumerate((rank_in, sens_in, grad_in)):
        arrived(src.at[pl.ds(0, n - 1)], all_send.at[k])


def on_device(x, w, e, b, sens, user_ids, slot_table, counts):
    me = lax.axis_index("dp")
    n = lax.axis_size("dp")
    x, e, b, sens = x[0], e[0], b[0, 0], sens[0]
    rows, depth = x.shape
    tok = rows // n
    cap = tok // 8
    adapters, _, width = e.shape
    features = b.shape[1]
    slots = n * cap
    owner, rank, slot = route(user_ids[0], slot_table[0], counts[0], n, cap)
    pick = (slot[:, None, :] == jnp.arange(slots, dtype=jnp.int32)[None, :, None]).astype(BF16)
    my_pick = lax.dynamic_index_in_dim(pick, me, 0, keepdims=False)
    send_sens = jnp.dot(my_pick, sens, preferred_element_type=F32).astype(BF16).reshape(n, cap, features)
    choose = owner.reshape(rows)[:, None] == jnp.arange(adapters, dtype=jnp.int32)[None, :]
    every = jnp.einsum("xz,szu->xsu", x, e, preferred_element_type=F32)
    part = jnp.sum(every * choose.astype(F32)[:, :, None], axis=1).astype(BF16)
    send_rank = jnp.einsum("sqr,srf->sqf", pick, part.reshape(n, tok, width), preferred_element_type=F32)
    send_rank = send_rank.astype(BF16).reshape(2, n // 2, n, cap, width).transpose(2, 1, 3, 0, 4)
    send_rank = send_rank.reshape(n, slots // 2, 2 * width)
    spot = (jnp.arange(n, dtype=jnp.int32)[:, None] % (n // 2) * cap + rank).reshape(rows)
    column = jnp.arange(slots, dtype=jnp.int32)
    aim = jnp.where(column < slots // 2, me, me + 1 - 2 * (me % 2))
    put = ((owner.reshape(rows)[:, None] == aim[None, :]) & (spot[:, None] == column[None, :] % (slots // 2))).astype(BF16)

    vmem = pl.BlockSpec(memory_space=pltpu.VMEM)
    wide = features // CORES // GROUPS
    hops = GROUPS * (UP + DOWN)
    chip_rows = rows // RING
    out, exit_grad, grads = pl.pallas_call(
        exchange,
        out_shape=(
            jax.ShapeDtypeStruct((tok, features), BF16),
            jax.ShapeDtypeStruct((width, features), F32),
            jax.ShapeDtypeStruct((n, slots // 2, 2 * width), BF16),
        ),
        in_specs=[vmem] * 6,
        out_specs=(vmem,) * 3,
        scratch_shapes=[
            pltpu.VMEM((rows, depth), BF16),
            pltpu.VMEM((2, GROUPS, depth, wide), BF16),
            pltpu.VMEM((width, features), BF16),
            pltpu.VMEM((GROUPS, 2 * width, wide), BF16),
            pltpu.VMEM((GROUPS, rows, wide), F32),
            pltpu.VMEM((n, slots // 2, 2 * width), BF16),
            pltpu.VMEM((slots // 2, 2 * width), F32),
            pltpu.VMEM((slots // 2, 2 * width), F32),
            pltpu.VMEM((rows, 2 * width), BF16),
            pltpu.VMEM((n, cap, features), BF16),
            pltpu.VMEM((slots // 2, 2 * width), BF16),
            pltpu.VMEM((n, slots // 2, 2 * width), BF16),
            pltpu.VMEM((hops, chip_rows, wide), BF16),
            pltpu.VMEM((hops, chip_rows, wide), BF16),
            pltpu.VMEM((GROUPS, tok, wide), BF16),
            pltpu.VMEM((GROUPS, tok, wide), BF16),
            pltpu.VMEM((slots, width), F32),
            pltpu.SemaphoreType.DMA((40,)),
            pltpu.SemaphoreType.DMA((40,)),
            pltpu.SemaphoreType.DMA((hops,)),
            pltpu.SemaphoreType.DMA((hops,)),
            pltpu.SemaphoreType.DMA((8,)),
            pltpu.SemaphoreType.DMA((8,)),
            pltpu.SemaphoreType.DMA((3,)),
            pltpu.SemaphoreType.DMA((3,)),
        ],
        compiler_params=pltpu.CompilerParams(
            collective_id=0, has_side_effects=True, vmem_limit_bytes=60 * 1024 * 1024
        ),
    )(x, w, b, send_rank, send_sens, put)

    grads = grads.reshape(n, n // 2, cap, 2, width).transpose(3, 1, 0, 2, 4).reshape(n, slots, width)
    grad_rows = jnp.einsum("sqr,sqf->srf", pick, grads, preferred_element_type=F32)
    grad_rows = grad_rows.reshape(rows, width).astype(BF16)
    entry_grad = jnp.einsum(
        "vg,vqh->qgh", x, choose.astype(BF16)[:, :, None] * grad_rows[:, None, :], preferred_element_type=F32
    )
    return out[None], entry_grad[None], exit_grad[None, None]


def solution(mesh):
    in_specs = (
        P("mp", None, "dp"),
        P("dp", "mp"),
        P("mp", None, "dp", None),
        P("mp", "dp", None, None),
        P("mp", "dp", None),
        P("mp", None),
        P("mp", None),
        P("mp", None),
    )
    out_specs = (P("mp", "dp", None), P("mp", None, "dp", None), P("mp", "dp", None, None))
    return jax.shard_map(on_device, mesh=mesh, in_specs=in_specs, out_specs=out_specs, check_vma=False)
```

time: 292 us -> 121 us (0.41)
  waiting for transfers between devices: 109 us -> 0 us
  Pallas kernels: 0 us -> 96.3 us
  blocking collectives: 75.7 us -> 0 us
  other arithmetic: 33.5 us -> 5.29 us
  matrix products: 29.2 us -> 11.3 us
  starting transfers between devices: 17.7 us -> 0 us
  between operations: 15.7 us -> 0.77 us
  local copies, waits for them, and re-layouts: 11.3 us -> 7.13 us
    pallas_call x0 -> x1, Pallas kernels: none -> 96.3 us  [on_device(): pl.pallas_call(exchange, out_shape=(jax.ShapeDtypeStruct((tok, features),...]
    all_gather x1 -> x0, blocking collectives: 75.7 us -> none  [on_device(): gathered = lax.all_gather(rank_grad[None], 'dp', axis=0, tiled=True)]
    all_gather x1 -> x0, waiting for transfers between devices: 74.1 us -> none  [on_device(): lax.all_gather(frozen_down_weight, 'mp', axis=1, tiled=True)]
    all_to_all x3 -> x0, waiting for transfers between devices: 33.7 us -> none  [the longest x1 28.3 us: on_device(): lax.all_to_all(send_grad, 'dp', split_axis=0, concat_axis=0, tiled=True)]
    all_to_all x3 -> x0, starting transfers between devices: 17.4 us -> none  [the longest x1 9.05 us: on_device(): lax.all_to_all(send_rank, 'dp', split_axis=0, concat_axis=0, tiled=True)]
    dot_general x8 -> x4, matrix products: 25.3 us -> 8.93 us  [the longest x1 5.78 us: on_device(): jnp.einsum('vg,vqh->qgh', x, choose.astype(BF16)[:, :, None] * grad_rows[...]
    scatter-add x2 -> x0, other arithmetic: 15.7 us -> none  [the longest x1 11 us: on_device(): rank_grad_rows = jnp.zeros((row_total, adapter_rank_width), jnp.float32)....]
    reduce_sum x4 -> x3, other arithmetic: 10.7 us -> 1.82 us  [the longest x1 0.79 us: route(): jnp.sum(jnp.where(user_ids[:, None] == ids[None, :], slot_table[None, :],...]
  transfers between devices with their start and end apart: 6 -> 0, of which waited for: 3 -> 0; matrix products, arithmetic and copies ran while one was open for 24% -> 0% of each run, Pallas kernels for 0% -> 0%
where the time goes in v1:
time: 121 us
  Pallas kernels  96.3 us (80%)
  matrix products  11.3 us (9%)
  local copies, waits for them, and re-layouts  7.13 us (6%)
  other arithmetic  5.29 us (4%)
    pallas_call x1, Pallas kernels, on_device(): pl.pallas_call(exchange, out_shape=(jax.ShapeDtypeStruct((tok, features),...  96.3 us
    dot_general x1, matrix products, on_device(): jnp.einsum('vg,vqh->qgh', x, choose.astype(BF16)[:, :, None] * grad_rows[...  5.78 us
    unnamed x10, local copies, waits for them, and re-layouts  3.26 us
    dot_general x1, matrix products, on_device(): jnp.dot(my_pick, sens, preferred_element_type=F32).astype(BF16)  2.49 us

profile of v1, /device:TPU:1, one launch (start us, length us, event | category | flops | bytes accessed | tf_op | source)
XLA Modules:
  0.0 120.8 jit_solution(4186892487499957755)
XLA Ops:
  0.7 1.5 %copy-done = bf16[1,16,896,64]{2,3,1,0:T(8,128)(2,1)S(1)} copy-done((bf16[1,16,896,64]{2,3,1,0:T(8,128)(2,1)S(1)}, bf16[1,16,896,64]{2,3,1,0:T(8,128)(2,1)}, u32[]{:S(2)}) %copy-start) | copy-done | bytes 1835032
  2.1 0.7 iota_compare_fusion.6
  3.0 0.8 select_reduce_fusion
  3.8 0.7 fusion.17
  4.6 0.5 convert_reduce_fusion
  5.1 0.7 broadcast_add_fusion
  5.9 0.2 iota_compare_fusion
  6.1 1.0 and_convert_fusion.put_ref
  7.2 2.5 %fusion.sens_ref = bf16[16,8,4096]{2,1,0:T(8,128)(2,1)} fusion(bf16[1,64,4096]{2,1,0:T(8,128)(2,1)} %param.12, pred[16,128,64]{1,2,0:T(32,128)(4,1)S(1)} %iota_compare_fusion, s32[]{:T(128)S(6)} %select_n.77), kind=kOutput, calls=%fused_computation.1 | convolution fusion | flops 67633152 | bytes 1581060 | tf_op jit(solution)/shard_map/dot_general | solution.py:357
  9.7 2.4 %fusion.20 = f32[1024,1024]{0,1:S(1)} fusion(bf16[896,1024]{0,1:T(8,128)(2,1)S(1)} %bitcast.41, bf16[1,1024,896]{2,1,0:T(8,128)(2,1)S(1)} %copy-done.1), kind=kOutput, calls=%fused_computation.36 | convolution fusion | flops 1879048192 | bytes 7864320
  12.0 0.5 multiply_reduce_fusion
  12.5 0.2 convert_element_type.47
  12.7 0.3 convolution_convert_fusion.2
  13.1 0.3 copy.21
  13.4 0.8 copy.22
  14.2 1.0 reshape.236.ranks_ref
  15.1 96.3 %shard_map.103 = (bf16[64,4096]{1,0:T(8,128)(2,1)}, f32[64,4096]{1,0:T(8,128)}, bf16[16,64,128]{2,1,0:T(8,128)(2,1)}) custom-call(bf16[1024,896]{1,0:T(8,128)(2,1)} %bitcast.45, bf16[896,256]{1,0:T(8,128)(2,1)} %w_ref.1, bf16[64,4096]{1,0:T(8,128)(2,1)} %bitcast.48, bf16[16,64,128]{2,1,0:T(8,128)(2,1)} %reshape.236.ranks_ref, ...), custom_call_target="tpu_custom_call" | custom-call | tf_op jit(solution)/shard_map/pallas_call | solution.py:373
  111.5 1.2 reshape.238
  112.7 0.1 copy.23
  112.8 0.3 convolution_convert_fusion.1
  113.1 0.1 copy.25
  113.3 5.8 %fusion.3 = f32[1,16,896,64]{2,3,1,0:T(8,128)} fusion(bf16[1,1024,896]{2,1,0:T(8,128)(2,1)} %param.8, bf16[1024,64]{0,1:T(8,128)(2,1)S(1)} %copy.25, bf16[1024,16]{0,1:T(8,128)(2,1)S(1)} %get-tuple-element.11), kind=kOutput, calls=%fused_computation.5 | convolution fusion | flops 1880096768 | bytes 5668864 | tf_op jit(solution)/shard_map/vg,vqh->qgh/dot_general | solution.py:417
  119.0 0.8 copy.33
  119.8 1.0 copy.34
  (15 shorter events, 0.3 us)
Async XLA Ops:
  0.6 1.5 %copy-start = (bf16[1,16,896,64]{2,3,1,0:T(8,128)(2,1)S(1)}, bf16[1,16,896,64]{2,3,1,0:T(8,128)(2,1)}, u32[]{:S(2)}) copy-start(bf16[1,16,896,64]{2,3,1,0:T(8,128)(2,1)} %param.10) | copy-start | bytes 5505028
  5.9 3.8 %copy-start.1 = (bf16[1,1024,896]{2,1,0:T(8,128)(2,1)S(1)}, bf16[1,1024,896]{2,1,0:T(8,128)(2,1)}, u32[]{:S(2)}) copy-start(bf16[1,1024,896]{2,1,0:T(8,128)(2,1)} %param.8) | copy-start | bytes 5505028
  113.2 5.8 %copy-start.3 = (bf16[64,4096]{1,0:T(8,128)(2,1)S(1)}, bf16[64,4096]{1,0:T(8,128)(2,1)}, u32[]{:S(2)}) copy-start(bf16[64,4096]{1,0:T(8,128)(2,1)} %get-tuple-element.6) | copy-start | bytes 1572868
  113.3 6.6 %copy-start.2 = (f32[64,4096]{1,0:T(8,128)S(1)}, f32[64,4096]{1,0:T(8,128)}, u32[]{:S(2)}) copy-start(f32[64,4096]{1,0:T(8,128)} %get-tuple-element.8) | copy-start | bytes 3145732

commit v2 on v1

v2 whole, which is shorter than its diff:
```python
import jax
import jax.numpy as jnp
from jax import lax
from jax.experimental import pallas as pl
from jax.experimental.pallas import tpu as pltpu
from jax.sharding import PartitionSpec as P

F32 = jnp.float32
BF16 = jnp.bfloat16
MESH = pl.DeviceIdType.MESH
SIDE = 4
RING = 8
CORES = 2
UP = (3, 4, 3, 4)
DOWN = (4, 3, 4, 3)
ORDER = [
    (0, 0), (1, 0), (3, 0), (0, 1),
    (0, 3), (1, 1), (3, 1), (1, 3),
    (3, 3), (2, 0), (0, 2), (1, 2),
    (2, 1), (2, 3), (3, 2), (2, 2),
]
GROUPS = 4
LANES = 128


def halved(part, offset):
    dx, dy = offset
    first, last = (dx, dy) if part == 0 else (dy, dx)
    return last == 2 or (last == 0 and first == 2)


def exchange(
    x_in, w_in, b_in, e_in, cotangent, users_ref, table_ref, counts_ref,
    out_ref, exit_ref, entry_ref,
    x_ref, w_ref, b_ref, e_ref, sens_ref, owner_ref, slot_ref, column_ref, ranks_out, sens_out,
    x_sib, w_all, b_sib, b_all, y_all, rank_in, rank_own, rank_sib, rank_rows, sens_in, grad_out, grad_in, grad_rows,
    part_out, part_in, last_out, last_in, grad_sum,
    ag_send, ag_recv, rs_send, rs_recv, pair_send, pair_recv, all_send, all_recv, load,
):
    n = RING * CORES
    dp = lax.axis_index("dp")
    mp = lax.axis_index("mp")
    z, c = dp // CORES, dp % CORES
    my_y, my_x = mp // SIDE, mp % SIDE
    sib = dp + 1 - 2 * c
    depth = w_ref.shape[0]
    half = depth // 2
    rows = x_ref.shape[0]
    chip_rows = rows // RING
    own_rows = chip_rows // CORES
    wide = LANES * (len(ORDER) // GROUPS)
    features = b_ref.shape[1]
    width = b_ref.shape[0]

    def at_x(sign):
        return my_y * SIDE + (my_x + SIDE + sign) % SIDE

    def at_y(sign):
        return ((my_y + SIDE + sign) % SIDE) * SIDE + my_x

    loads = [
        pltpu.make_async_copy(src, dst, load.at[k])
        for k, (src, dst) in enumerate(
            ((cotangent, sens_ref), (w_in, w_ref), (x_in, x_ref), (b_in, b_ref), (e_in, e_ref))
        )
    ]
    for copy in loads:
        copy.start()

    barrier = pltpu.get_barrier_semaphore()
    for k in range(1, n):
        pl.semaphore_signal(barrier, inc=1, device_id={"dp": (dp + k) % n}, device_id_type=MESH)
    for to in (at_x(1), at_x(-1), at_y(1), at_y(-1)):
        pl.semaphore_signal(barrier, inc=1, device_id={"mp": to}, device_id_type=MESH)

    adapters = n
    seg = rows // n
    cap = seg // 8
    blocks = rows // LANES
    users = users_ref[...]
    line = lax.broadcasted_iota(jnp.int32, users.shape, 0)
    lane = lax.broadcasted_iota(jnp.int32, users.shape, 1)
    upper = lane >= seg
    storage = jnp.zeros_like(users)
    limit = jnp.zeros_like(users)
    for k in range(n):
        storage = jnp.where(users == k, table_ref[k], storage)
        limit = jnp.where((line == k // CORES) & (upper == bool(k % CORES)), counts_ref[k], limit)
    owner = jnp.where(jnp.where(upper, lane - seg, lane) < limit, storage, -1)
    ids = lax.broadcasted_iota(jnp.int32, (adapters, LANES), 0)
    hot = jnp.concatenate([jnp.where(owner[k : k + 1] == ids, 1.0, 0.0) for k in range(blocks)], axis=0)
    r0 = lax.broadcasted_iota(jnp.int32, (LANES, LANES), 0)
    r1 = lax.broadcasted_iota(jnp.int32, (LANES, LANES), 1)
    before_me = jnp.where((r0 < r1) & ((r0 >= seg) == (r1 >= seg)), 1.0, 0.0).astype(BF16)
    count = jnp.dot(hot.astype(BF16), before_me, preferred_element_type=F32)
    order = jnp.sum((hot * count).reshape(blocks, adapters, LANES), axis=1)
    slot = jnp.where(owner < 0, -1.0, owner.astype(F32) * cap + order)
    spot = order + (line * cap + jnp.where(upper, seg, 0)).astype(F32)
    column = jnp.where(owner == dp, spot, jnp.where(owner == sib, spot + LANES, -1.0))
    owner_ref[...] = owner
    slot_ref[...] = slot
    column_ref[...] = column
    slot_ids = lax.broadcasted_iota(jnp.int32, (LANES, LANES), 0).astype(F32)
    in_upper = r1 >= seg

    def pick(k):
        return jnp.where(slot_ref[pl.ds(k, 1), :] == slot_ids, 1.0, 0.0).astype(BF16)

    loads[0].wait()
    one_hot = jnp.where((slot_ref[pl.ds(z, 1), :] == slot_ids) & (in_upper == (c == 1)), 1.0, 0.0).astype(BF16)

    @pl.loop(0, features // wide)
    def _(i):
        at = pl.ds(pl.multiple_of(i * wide, wide), wide)
        block = sens_ref[:, at]
        chosen = jnp.dot(one_hot, jnp.concatenate([block, block], axis=0), preferred_element_type=F32)
        sens_out[:, :, at] = chosen.reshape(n, cap, wide).astype(BF16)

    for copy in loads[1:4]:
        copy.wait()
    pl.semaphore_wait(barrier, n - 1 + 4)

    sent = []

    def send(src, dst, send_sem, recv_sem, to):
        copy = pltpu.make_async_remote_copy(
            src_ref=src, dst_ref=dst, send_sem=send_sem, recv_sem=recv_sem, device_id=to, device_id_type=MESH
        )
        copy.start()
        sent.append(copy)

    def arrived(dst, sem):
        pltpu.make_async_copy(dst, dst, sem).wait()

    names = {}

    def sem_of(part, offset, piece):
        return names.setdefault((part, offset, piece), len(names))

    def place(part, offset, piece=None):
        spot = ORDER.index(offset)
        cols = pl.ds(LANES * (spot % GROUPS), LANES)
        if piece is None:
            return w_all.at[part, spot // GROUPS, :, cols]
        return w_all.at[part, spot // GROUPS, pl.ds(half * piece, half), cols]

    def pass_on(axis, sign, part, offset, piece=None, src=None):
        dx, dy = offset
        seen = ((dx - sign) % SIDE, dy) if axis == "x" else (dx, (dy - sign) % SIDE)
        to = at_x(sign) if axis == "x" else at_y(sign)
        if src is None:
            src = place(part, offset, piece)
        num = sem_of(part, seen, piece)
        send(src, place(part, seen, piece), ag_send.at[num], ag_recv.at[num], {"mp": to})

    def got(part, offset):
        for piece in (0, 1) if halved(part, offset) else (None,):
            arrived(place(part, offset, piece), ag_recv.at[sem_of(part, offset, piece)])

    def both(axis, part, offset, src=None):
        for sign in (1, -1):
            pass_on(axis, sign, part, offset, None, src)

    def relay(axis, part, offset):
        away = offset[0] if axis == "x" else offset[1]
        if away == 1:
            pass_on(axis, -1, part, offset, 0)
        else:
            pass_on(axis, 1, part, offset, 1)

    own_cols = w_ref.at[:, pl.ds(pl.multiple_of(LANES * c, LANES), LANES)]
    sib_cols = w_ref.at[:, pl.ds(pl.multiple_of(LANES * (1 - c), LANES), LANES)]
    send(sib_cols, place(1, (0, 0)), pair_send.at[0], pair_recv.at[0], {"dp": sib})
    both("x", 0, (0, 0), own_cols)
    both("y", 0, (0, 0), own_cols)

    def to_all(sem, src_of, dst, spans):
        def body(k, _):
            to = (dp + k) % n
            pltpu.make_async_remote_copy(
                src_ref=src_of(to), dst_ref=dst.at[dp], send_sem=all_send.at[sem], recv_sem=all_recv.at[sem],
                device_id={"dp": to}, device_id_type=MESH,
            ).start()
            return 0
        for first, last in spans:
            lax.fori_loop(first, last, body, 0)

    def all_done(sem, dst):
        arrived(dst.at[pl.ds(0, n - 1)], all_recv.at[sem])

    to_all(1, lambda to: sens_out.at[to], sens_in, ((5, 7), (10, 12)))
    send(x_ref, x_sib, pair_send.at[1], pair_recv.at[1], {"dp": sib})
    send(b_ref, b_sib, pair_send.at[2], pair_recv.at[2], {"dp": sib})
    w_all[0, 0, :, 0:LANES] = own_cols[...]
    sens_in[dp] = sens_out[dp]
    arrived(place(1, (0, 0)), pair_recv.at[0])
    both("y", 1, (0, 0))
    both("x", 1, (0, 0))

    loads[4].wait()

    @pl.loop(0, blocks // 2)
    def _(i):
        tile = 2 * LANES
        every = lax.dot_general(
            e_ref[...], x_ref[pl.ds(pl.multiple_of(i * tile, tile), tile)], (((1,), (1,)), ((), ())),
            preferred_element_type=F32,
        )
        own = jnp.concatenate([owner_ref[pl.ds(2 * i, 1), :], owner_ref[pl.ds(2 * i + 1, 1), :]], axis=1)
        ranks = jnp.zeros((width, tile), F32)
        for k in range(adapters):
            ranks = ranks + jnp.where(own == k, every[k * width : (k + 1) * width], 0.0)
        for j in range(2):
            piece = ranks[:, j * LANES : (j + 1) * LANES]
            low = lax.broadcasted_iota(jnp.int32, piece.shape, 1) < seg
            spread = jnp.concatenate([jnp.where(low, piece, 0.0), jnp.where(low, 0.0, piece)], axis=0).astype(BF16)
            placed = lax.dot_general(pick(2 * i + j), spread, (((1,), (1,)), ((), ())), preferred_element_type=F32)
            ranks_out[:, pl.ds(2 * i + j, 1)] = placed.reshape(n, 1, cap, 2 * width).astype(BF16)

    to_all(0, lambda to: ranks_out.at[to], rank_in, ((1, n),))
    to_all(1, lambda to: sens_out.at[to], sens_in, ((1, 5), (7, 10), (12, n)))
    rank_in[dp] = ranks_out[dp]

    for d in ((1, 0), (3, 0)):
        got(0, d)
        both("y", 0, d)
        relay("x", 0, d)
    for e in ((0, 1), (0, 3)):
        got(1, e)
        both("x", 1, e)
        relay("y", 1, e)

    for d in ((1, 0), (3, 0)):
        e = (d[1], d[0])
        got(1, d)
        relay("x", 1, d)
        got(0, e)
        relay("y", 0, e)

    arrived(b_sib, pair_recv.at[2])
    for g in range(GROUPS):
        for j in range(GROUPS):
            dx, dy = ORDER[g * GROUPS + j]
            m = ((my_y + dy) % SIDE) * SIDE + (my_x + dx) % SIDE
            col = pl.ds(pl.multiple_of(m * CORES * LANES + c * LANES, LANES), LANES)
            b_all[g, 0:width, j * LANES : (j + 1) * LANES] = b_ref[:, col]
            b_all[g, width : 2 * width, j * LANES : (j + 1) * LANES] = b_sib[:, col]
    all_done(0, rank_in)
    total = rank_in[0].astype(F32)
    for k in range(1, n):
        total = total + rank_in[k].astype(F32)
    rank_own[...] = total.reshape(rank_own.shape)
    send(rank_own, rank_sib, pair_send.at[3], pair_recv.at[3], {"dp": sib})
    arrived(rank_sib, pair_recv.at[3])
    mine, theirs = rank_own[...], rank_sib[...]
    low = lax.broadcasted_iota(jnp.int32, mine.shape, 1) < width
    stack = jnp.concatenate(
        [
            jnp.where(low, mine, 0.0),
            jnp.where(low, pltpu.roll(mine, width, 1), 0.0),
            jnp.where(low, 0.0, pltpu.roll(theirs, width, 1)),
            jnp.where(low, 0.0, theirs),
        ],
        axis=0,
    ).astype(BF16)

    @pl.loop(0, blocks)
    def _(k):
        put = lax.broadcasted_iota(jnp.int32, (2 * LANES, LANES), 0).astype(F32) == column_ref[pl.ds(k, 1), :]
        put = jnp.where(put, 1.0, 0.0).astype(BF16)
        rank_rows[pl.ds(pl.multiple_of(k * LANES, LANES), LANES)] = lax.dot_general(
            put, stack, (((0,), (0,)), ((), ())), preferred_element_type=F32
        ).astype(BF16)

    arrived(x_sib, pair_recv.at[1])

    def product(g):
        tile = rows // 4

        @pl.loop(0, 4)
        def _(i):
            at = pl.ds(pl.multiple_of(i * tile, tile), tile)
            y_all[g, at] = (
                jnp.dot(x_ref[at], w_all[0, g], preferred_element_type=F32)
                + jnp.dot(x_sib[at], w_all[1, g], preferred_element_type=F32)
                + jnp.dot(rank_rows[at], b_all[g], preferred_element_type=F32)
            )

    def sem_rs(g, way, step):
        return g * (RING - 1) + (step - 1 if way > 0 else UP[g] + step - 1)

    def hop(g, step):
        for way, length in ((-1, DOWN[g]), (1, UP[g])):
            if step > length:
                continue
            dest = (z + RING + way * (length + 1 - step)) % RING
            value = y_all[g, pl.ds(pl.multiple_of(dest * chip_rows, chip_rows), chip_rows)]
            if step > 1:
                before = sem_rs(g, way, step - 1)
                arrived(part_in.at[before], rs_recv.at[before])
                value = value + part_in[before].astype(F32)
            num = sem_rs(g, way, step)
            part_out[num] = value.astype(BF16)
            to = ((z + RING + way) % RING) * CORES + c
            send(part_out.at[num], part_in.at[num], rs_send.at[num], rs_recv.at[num], {"dp": to})

    def store(value, g, core):
        for j in range(GROUPS):
            dx, dy = ORDER[g * GROUPS + j]
            m = ((my_y + dy) % SIDE) * SIDE + (my_x + dx) % SIDE
            col = pl.ds(pl.multiple_of(m * CORES * LANES + core * LANES, LANES), LANES)
            out_ref[:, col] = value[:, j * LANES : (j + 1) * LANES]

    def finish(g):
        up, down = sem_rs(g, 1, UP[g]), sem_rs(g, -1, DOWN[g])
        arrived(part_in.at[up], rs_recv.at[up])
        arrived(part_in.at[down], rs_recv.at[down])

        def rows_of(core):
            part = pl.ds(pl.multiple_of(core * own_rows, own_rows), own_rows)
            base = y_all[g, pl.ds(pl.multiple_of(z * chip_rows + core * own_rows, own_rows), own_rows)]
            return (base + part_in[up, part].astype(F32) + part_in[down, part].astype(F32)).astype(BF16)

        last_out[g] = rows_of(1 - c)
        send(last_out.at[g], last_in.at[g], pair_send.at[4 + g], pair_recv.at[4 + g], {"dp": sib})
        store(rows_of(c), g, c)

    def close(g):
        arrived(last_in.at[g], pair_recv.at[4 + g])
        store(last_in[g], g, 1 - c)

    def exit_and_rank_gradients():
        all_done(1, sens_in)
        mine = rank_own[...]
        halves = [mine[:, k * width : (k + 1) * width].reshape(blocks, 1, cap, width) for k in range(2)]
        ranks = jnp.concatenate(halves, axis=1).reshape(n * cap, width).astype(BF16)
        grad_sum[...] = jnp.zeros_like(grad_sum)

        @pl.loop(0, features // wide)
        def _(i):
            at = pl.ds(pl.multiple_of(i * wide, wide), wide)
            block = sens_in[:, :, at].astype(F32).reshape(n * cap, wide).astype(BF16)
            exit_ref[:, at] = lax.dot_general(ranks, block, (((0,), (0,)), ((), ())), preferred_element_type=F32)
            grad_sum[...] += lax.dot_general(
                block, b_ref[:, at], (((1,), (1,)), ((), ())), preferred_element_type=F32
            )

        grad = grad_sum[...].reshape(blocks, 2, cap, width)
        halves = [grad[:, k].reshape(blocks * cap, width) for k in range(2)]
        grad_out[...] = jnp.concatenate(halves, axis=1).reshape(blocks, cap, 2 * width).astype(BF16)
        to_all(2, lambda to: grad_out, grad_in, ((1, n),))
        grad_in[dp] = grad_out[...]

    def spread_gradients():
        all_done(2, grad_in)

        @pl.loop(0, blocks)
        def _(k):
            block = grad_in[:, pl.ds(k, 1)].astype(F32).reshape(n * cap, 2 * width).astype(BF16)
            both_halves = lax.dot_general(block, pick(k), (((0,), (0,)), ((), ())), preferred_element_type=F32)
            low = lax.broadcasted_iota(jnp.int32, (width, LANES), 1) < seg
            grads = jnp.where(low, both_halves[0:width], both_halves[width : 2 * width])
            own = owner_ref[pl.ds(k, 1), :]
            at = pl.ds(pl.multiple_of(k * LANES, LANES), LANES)
            for u in range(adapters):
                grad_rows[u * width : (u + 1) * width, at] = jnp.where(own == u, grads, 0.0).astype(BF16)

    def entry_gradient(i):
        tile = adapters * width // 4
        at = slice(i * tile, (i + 1) * tile)
        entry_ref[at] = jnp.dot(grad_rows[at], x_ref[...], preferred_element_type=F32)

    product(0)
    hop(0, 1)
    for d in ((1, 1), (3, 1), (1, 3), (3, 3)):
        got(1, d)
        relay("x", 1, d)
        e = (d[1], d[0])
        got(0, e)
        relay("y", 0, e)
    got(0, (2, 0))
    both("y", 0, (2, 0))
    got(1, (0, 2))
    both("x", 1, (0, 2))
    product(1)
    hop(1, 1)
    hop(0, 2)
    for d in ((1, 2), (3, 2)):
        got(1, d)
        relay("x", 1, d)
        e = (d[1], d[0])
        got(0, e)
        relay("y", 0, e)
    hop(0, 3)
    hop(1, 2)
    exit_and_rank_gradients()
    for part in (0, 1):
        for d in ((2, 0), (0, 2), (1, 2)):
            if (part, d) not in ((0, (2, 0)), (1, (0, 2)), (1, (1, 2))):
                got(part, d)
    product(2)
    hop(2, 1)
    hop(1, 3)
    hop(0, 4)
    for part in (0, 1):
        for d in ((2, 1), (2, 3), (3, 2), (2, 2)):
            if (part, d) not in ((0, (2, 1)), (0, (2, 3)), (1, (3, 2))):
                got(part, d)
    product(3)
    hop(3, 1)
    hop(2, 2)
    hop(1, 4)
    finish(0)
    spread_gradients()
    hop(3, 2)
    hop(2, 3)
    finish(1)
    entry_gradient(0)
    entry_gradient(1)
    hop(3, 3)
    hop(2, 4)
    entry_gradient(2)
    entry_gradient(3)
    hop(3, 4)
    close(0)
    close(1)
    finish(2)
    close(2)
    finish(3)
    close(3)

    for copy in sent:
        copy.wait_send()
    for k, src in enumerate((rank_in, sens_in, grad_in)):
        arrived(src.at[pl.ds(0, n - 1)], all_send.at[k])


def on_device(x, w, e, b, sens, user_ids, slot_table, counts):
    n = lax.axis_size("dp")
    x, e, b, sens = x[0], e[0], b[0, 0], sens[0]
    rows, depth = x.shape
    tok = rows // n
    cap = tok // 8
    adapters, _, width = e.shape
    features = b.shape[1]
    slots = n * cap
    blocks = rows // LANES
    wide = features // CORES // GROUPS
    hops = GROUPS * (RING - 1)
    chip_rows = rows // RING
    vmem = pl.BlockSpec(memory_space=pltpu.VMEM)
    smem = pl.BlockSpec(memory_space=pltpu.SMEM)
    out, exit_grad, entry_grad = pl.pallas_call(
        exchange,
        out_shape=(
            jax.ShapeDtypeStruct((tok, features), BF16),
            jax.ShapeDtypeStruct((width, features), F32),
            jax.ShapeDtypeStruct((adapters * width, depth), F32),
        ),
        in_specs=[pl.BlockSpec(memory_space=pl.ANY)] * 5 + [vmem] + [smem] * 2,
        out_specs=(vmem,) * 3,
        scratch_shapes=[
            pltpu.VMEM((rows, depth), BF16),
            pltpu.VMEM(w.shape, BF16),
            pltpu.VMEM((width, features), BF16),
            pltpu.VMEM((adapters * width, depth), BF16),
            pltpu.VMEM((tok, features), BF16),
            pltpu.VMEM((blocks, LANES), jnp.int32),
            pltpu.VMEM((blocks, LANES), F32),
            pltpu.VMEM((blocks, LANES), F32),
            pltpu.VMEM((n, blocks, cap, 2 * width), BF16),
            pltpu.VMEM((n, cap, features), BF16),
            pltpu.VMEM((rows, depth), BF16),
            pltpu.VMEM((2, GROUPS, depth, wide), BF16),
            pltpu.VMEM((width, features), BF16),
            pltpu.VMEM((GROUPS, 2 * width, wide), BF16),
            pltpu.VMEM((GROUPS, rows, wide), F32),
            pltpu.VMEM((n, blocks, cap, 2 * width), BF16),
            pltpu.VMEM((slots // 2, 2 * width), F32),
            pltpu.VMEM((slots // 2, 2 * width), F32),
            pltpu.VMEM((rows, 2 * width), BF16),
            pltpu.VMEM((n, cap, features), BF16),
            pltpu.VMEM((blocks, cap, 2 * width), BF16),
            pltpu.VMEM((n, blocks, cap, 2 * width), BF16),
            pltpu.VMEM((adapters * width, rows), BF16),
            pltpu.VMEM((hops, chip_rows, wide), BF16),
            pltpu.VMEM((hops, chip_rows, wide), BF16),
            pltpu.VMEM((GROUPS, tok, wide), BF16),
            pltpu.VMEM((GROUPS, tok, wide), BF16),
            pltpu.VMEM((slots, width), F32),
            pltpu.SemaphoreType.DMA((40,)),
            pltpu.SemaphoreType.DMA((40,)),
            pltpu.SemaphoreType.DMA((hops,)),
            pltpu.SemaphoreType.DMA((hops,)),
            pltpu.SemaphoreType.DMA((8,)),
            pltpu.SemaphoreType.DMA((8,)),
            pltpu.SemaphoreType.DMA((3,)),
            pltpu.SemaphoreType.DMA((3,)),
            pltpu.SemaphoreType.DMA((5,)),
        ],
        compiler_params=pltpu.CompilerParams(
            collective_id=0, has_side_effects=True, vmem_limit_bytes=62 * 1024 * 1024
        ),
    )(
        x,
        w,
        b,
        e.transpose(0, 2, 1).reshape(adapters * width, depth),
        sens,
        user_ids.reshape(blocks, LANES),
        slot_table[0],
        counts[0],
    )
    entry_grad = entry_grad.reshape(adapters, width, depth).transpose(0, 2, 1)
    return out[None], entry_grad[None], exit_grad[None, None]


def solution(mesh):
    in_specs = (
        P("mp", None, "dp"),
        P("dp", "mp"),
        P("mp", None, "dp", None),
        P("mp", "dp", None, None),
        P("mp", "dp", None),
        P("mp", None),
        P("mp", None),
        P("mp", None),
    )
    out_specs = (P("mp", "dp", None), P("mp", None, "dp", None), P("mp", "dp", None, None))
    return jax.shard_map(on_device, mesh=mesh, in_specs=in_specs, out_specs=out_specs, check_vma=False)
```

time: 121 us -> 103 us (0.85)
  matrix products: 11.3 us -> 0 us
  other arithmetic: 5.29 us -> 0 us
  Pallas kernels: 96.3 us -> 94.7 us
    dot_general x4 -> x0, matrix products: 8.93 us -> none  [the longest x1 5.78 us: on_device(): jnp.einsum('vg,vqh->qgh', x, choose.astype(BF16)[:, :, None] * grad_rows[...]
    unnamed x10 -> x5, local copies, waits for them, and re-layouts: 3.26 us -> 7.17 us
    unnamed x1 -> x0, matrix products: 2.36 us -> none
    reshape x4 -> x0, local copies, waits for them, and re-layouts: 2.31 us -> none  [the longest x2 1.29 us: on_device(): grads.reshape(n, n // 2, cap, 2, width).transpose(3, 1, 0, 2, 4)]
    reduce_sum x3 -> x0, other arithmetic: 1.82 us -> none  [the longest x1 0.79 us: route(): jnp.sum(jnp.where(user_ids[:, None] == ids[None, :], slot_table[None, :],...]
    pallas_call x1, Pallas kernels: 96.3 us -> 94.7 us  [on_device(): pl.pallas_call(exchange, out_shape=(jax.ShapeDtypeStruct((tok, features),...]
where the time goes in v2:
time: 103 us
  Pallas kernels  94.7 us (92%)
  local copies, waits for them, and re-layouts  7.17 us (7%)
    pallas_call x1, Pallas kernels, on_device(): pl.pallas_call(exchange, out_shape=(jax.ShapeDtypeStruct((tok, features),...  94.7 us
    unnamed x5, local copies, waits for them, and re-layouts  7.17 us

profile of v2, /device:TPU:1, one launch (start us, length us, event | category | flops | bytes accessed | tf_op | source)
XLA Modules:
  0.0 102.5 jit_solution(1604753881132688894)
XLA Ops:
  0.6 94.7 %shard_map.103 = (bf16[64,4096]{1,0:T(8,128)(2,1)}, f32[64,4096]{1,0:T(8,128)}, f32[1024,896]{1,0:T(8,128)}) custom-call(bf16[1024,896]{1,0:T(8,128)(2,1)} %bitcast.19, bf16[896,256]{1,0:T(8,128)(2,1)} %w_in.1, bf16[64,4096]{1,0:T(8,128)(2,1)} %bitcast.22, bf16[1024,896]{1,0:T(8,128)(2,1)} %bitcast.20, bf16[64,4096]{1,0:T(8,128)(2,1)} %bitcast.23, ...), custom_call_target="tpu_custom_call" | custom-call | tf_op jit(solution)/shard_map/pallas_call | solution.py:453
  95.3 1.9 %copy.14 = bf16[1,64,4096]{2,1,0:T(8,128)(2,1)} copy(bf16[1,64,4096]{2,1,0:T(8,128)(2,1)} %bitcast.24) | data formatting | bytes 1048576
  97.2 0.0 copy-start
  97.2 4.3 %copy.15 = f32[1,16,896,64]{2,3,1,0:T(8,128)} copy(f32[1,16,896,64]{2,3,1,0:T(8,128)} %bitcast.18) | data formatting | bytes 7340032
  101.5 0.0 copy-done
  101.5 1.0 copy.16
Async XLA Ops:
  97.2 4.3 %copy-start = (f32[64,4096]{1,0:T(8,128)S(1)}, f32[64,4096]{1,0:T(8,128)}, u32[]{:S(2)}) copy-start(f32[64,4096]{1,0:T(8,128)} %get-tuple-element.8) | copy-start | bytes 3145732

commit v3 on v2

--- a/solution.py
+++ b/solution.py
@@ -33,9 +33,9 @@
     x_in, w_in, b_in, e_in, cotangent, users_ref, table_ref, counts_ref,
     out_ref, exit_ref, entry_ref,
     x_ref, w_ref, b_ref, e_ref, sens_ref, owner_ref, slot_ref, column_ref, ranks_out, sens_out,
-    x_sib, w_all, b_sib, b_all, y_all, rank_in, rank_own, rank_sib, rank_rows, sens_in, grad_out, grad_in, grad_rows,
-    part_out, part_in, last_out, last_in, grad_sum,
-    ag_send, ag_recv, rs_send, rs_recv, pair_send, pair_recv, all_send, all_recv, load,
+    x_sib, w_all, b_sib, b_all, y_all, rank_pair, pair_sum, rank_in, rank_own, rank_sib, rank_rows, sens_in, grad_out, grad_in, grad_rows,
+    part_out, part_in, near_out, near_in, last_in, grad_sum,
+    ag_send, ag_recv, rs_send, rs_recv, pair_send, pair_recv, all_send, all_recv, load, last_send, last_recv,
 ):
     n = RING * CORES
     dp = lax.axis_index("dp")
@@ -168,12 +168,6 @@
         else:
             pass_on(axis, 1, part, offset, 1)
 
-    own_cols = w_ref.at[:, pl.ds(pl.multiple_of(LANES * c, LANES), LANES)]
-    sib_cols = w_ref.at[:, pl.ds(pl.multiple_of(LANES * (1 - c), LANES), LANES)]
-    send(sib_cols, place(1, (0, 0)), pair_send.at[0], pair_recv.at[0], {"dp": sib})
-    both("x", 0, (0, 0), own_cols)
-    both("y", 0, (0, 0), own_cols)
-
     def to_all(sem, src_of, dst, spans):
         def body(k, _):
             to = (dp + k) % n
@@ -185,16 +179,29 @@
         for first, last in spans:
             lax.fori_loop(first, last, body, 0)
 
-    def all_done(sem, dst):
-        arrived(dst.at[pl.ds(0, n - 1)], all_recv.at[sem])
+    def to_chips(sem, src_of, dst):
+        def body(k, _):
+            to = (z + k) % RING
+            pltpu.make_async_remote_copy(
+                src_ref=src_of(to), dst_ref=dst, send_sem=all_send.at[sem], recv_sem=all_recv.at[sem],
+                device_id={"dp": to * CORES + c}, device_id_type=MESH,
+            ).start()
+            return 0
+        lax.fori_loop(1, RING, body, 0)
 
     to_all(1, lambda to: sens_out.at[to], sens_in, ((5, 7), (10, 12)))
+
+    own_cols = w_ref.at[:, pl.ds(pl.multiple_of(LANES * c, LANES), LANES)]
+    sib_cols = w_ref.at[:, pl.ds(pl.multiple_of(LANES * (1 - c), LANES), LANES)]
+    send(sib_cols, place(1, (0, 0)), pair_send.at[0], pair_recv.at[0], {"dp": sib})
+    both("x", 0, (0, 0), own_cols)
     send(x_ref, x_sib, pair_send.at[1], pair_recv.at[1], {"dp": sib})
     send(b_ref, b_sib, pair_send.at[2], pair_recv.at[2], {"dp": sib})
     w_all[0, 0, :, 0:LANES] = own_cols[...]
     sens_in[dp] = sens_out[dp]
     arrived(place(1, (0, 0)), pair_recv.at[0])
     both("y", 1, (0, 0))
+    both("y", 0, (0, 0), own_cols)
     both("x", 1, (0, 0))
 
     loads[4].wait()
@@ -215,11 +222,16 @@
             low = lax.broadcasted_iota(jnp.int32, piece.shape, 1) < seg
             spread = jnp.concatenate([jnp.where(low, piece, 0.0), jnp.where(low, 0.0, piece)], axis=0).astype(BF16)
             placed = lax.dot_general(pick(2 * i + j), spread, (((1,), (1,)), ((), ())), preferred_element_type=F32)
-            ranks_out[:, pl.ds(2 * i + j, 1)] = placed.reshape(n, 1, cap, 2 * width).astype(BF16)
-
-    to_all(0, lambda to: ranks_out.at[to], rank_in, ((1, n),))
+            placed = placed.reshape(RING, CORES, 1, cap, 2 * width).astype(BF16)
+            for core in range(CORES):
+                ranks_out[core, :, pl.ds(2 * i + j, 1)] = placed[:, core]
+
+    send(ranks_out.at[1 - c], rank_pair, pair_send.at[8], pair_recv.at[8], {"dp": sib})
+    arrived(rank_pair, pair_recv.at[8])
+    pair_sum[...] = (ranks_out[c].astype(F32) + rank_pair[...].astype(F32)).astype(BF16)
+    to_chips(0, lambda to: pair_sum.at[to], rank_in.at[z])
     to_all(1, lambda to: sens_out.at[to], sens_in, ((1, 5), (7, 10), (12, n)))
-    rank_in[dp] = ranks_out[dp]
+    rank_in[z] = pair_sum[z]
 
     for d in ((1, 0), (3, 0)):
         got(0, d)
@@ -245,9 +257,9 @@
             col = pl.ds(pl.multiple_of(m * CORES * LANES + c * LANES, LANES), LANES)
             b_all[g, 0:width, j * LANES : (j + 1) * LANES] = b_ref[:, col]
             b_all[g, width : 2 * width, j * LANES : (j + 1) * LANES] = b_sib[:, col]
-    all_done(0, rank_in)
+    arrived(rank_in.at[pl.ds(0, RING - 1)], all_recv.at[0])
     total = rank_in[0].astype(F32)
-    for k in range(1, n):
+    for k in range(1, RING):
         total = total + rank_in[k].astype(F32)
     rank_own[...] = total.reshape(rank_own.shape)
     send(rank_own, rank_sib, pair_send.at[3], pair_recv.at[3], {"dp": sib})
@@ -301,8 +313,15 @@
                 value = value + part_in[before].astype(F32)
             num = sem_rs(g, way, step)
             part_out[num] = value.astype(BF16)
-            to = ((z + RING + way) % RING) * CORES + c
-            send(part_out.at[num], part_in.at[num], rs_send.at[num], rs_recv.at[num], {"dp": to})
+            to = ((z + RING + way) % RING) * CORES
+            if step < length:
+                send(part_out.at[num], part_in.at[num], rs_send.at[num], rs_recv.at[num], {"dp": to + c})
+                continue
+            side = (1 + way) // 2
+            for core in range(CORES):
+                piece = part_out.at[num, pl.ds(core * own_rows, own_rows)]
+                out_sem = last_send.at[g * 4 + side * 2 + core]
+                send(piece, last_in.at[g, side, c], out_sem, last_recv.at[g * 4 + side * 2 + c], {"dp": to + core})
 
     def store(value, g, core):
         for j in range(GROUPS):
@@ -311,26 +330,30 @@
             col = pl.ds(pl.multiple_of(m * CORES * LANES + core * LANES, LANES), LANES)
             out_ref[:, col] = value[:, j * LANES : (j + 1) * LANES]
 
+    def rows_of(g, core):
+        return y_all[g, pl.ds(pl.multiple_of(z * chip_rows + core * own_rows, own_rows), own_rows)]
+
+    def lend(g):
+        near_out[g] = rows_of(g, 1 - c).astype(BF16)
+        send(near_out.at[g], near_in.at[g], pair_send.at[4 + g], pair_recv.at[4 + g], {"dp": sib})
+
     def finish(g):
-        up, down = sem_rs(g, 1, UP[g]), sem_rs(g, -1, DOWN[g])
-        arrived(part_in.at[up], rs_recv.at[up])
-        arrived(part_in.at[down], rs_recv.at[down])
-
-        def rows_of(core):
-            part = pl.ds(pl.multiple_of(core * own_rows, own_rows), own_rows)
-            base = y_all[g, pl.ds(pl.multiple_of(z * chip_rows + core * own_rows, own_rows), own_rows)]
-            return (base + part_in[up, part].astype(F32) + part_in[down, part].astype(F32)).astype(BF16)
-
-        last_out[g] = rows_of(1 - c)
-        send(last_out.at[g], last_in.at[g], pair_send.at[4 + g], pair_recv.at[4 + g], {"dp": sib})
-        store(rows_of(c), g, c)
-
-    def close(g):
-        arrived(last_in.at[g], pair_recv.at[4 + g])
-        store(last_in[g], g, 1 - c)
+        arrived(near_in.at[g], pair_recv.at[4 + g])
+        for side in range(2):
+            for core in range(CORES):
+                arrived(last_in.at[g, side, core], last_recv.at[g * 4 + side * 2 + core])
+        value = rows_of(g, c) + last_in[g, 0, c].astype(F32) + last_in[g, 1, c].astype(F32)
+        store(value.astype(BF16), g, c)
+        value = near_in[g].astype(F32) + last_in[g, 0, 1 - c].astype(F32) + last_in[g, 1, 1 - c].astype(F32)
+        store(value.astype(BF16), g, 1 - c)
+
+    def drain(count):
+        for copy in sent[:count]:
+            copy.wait_send()
+        del sent[:count]
 
     def exit_and_rank_gradients():
-        all_done(1, sens_in)
+        arrived(sens_in.at[pl.ds(0, n - 1)], all_recv.at[1])
         mine = rank_own[...]
         halves = [mine[:, k * width : (k + 1) * width].reshape(blocks, 1, cap, width) for k in range(2)]
         ranks = jnp.concatenate(halves, axis=1).reshape(n * cap, width).astype(BF16)
@@ -348,15 +371,20 @@
         grad = grad_sum[...].reshape(blocks, 2, cap, width)
         halves = [grad[:, k].reshape(blocks * cap, width) for k in range(2)]
         grad_out[...] = jnp.concatenate(halves, axis=1).reshape(blocks, cap, 2 * width).astype(BF16)
-        to_all(2, lambda to: grad_out, grad_in, ((1, n),))
-        grad_in[dp] = grad_out[...]
+        to_chips(2, lambda to: grad_out, grad_in.at[c, z])
+        grad_in[c, z] = grad_out[...]
+
+    def swap_gradients():
+        arrived(grad_in.at[0, pl.ds(0, RING - 1)], all_recv.at[2])
+        send(grad_in.at[c], grad_in.at[c], pair_send.at[9], pair_recv.at[9], {"dp": sib})
 
     def spread_gradients():
-        all_done(2, grad_in)
+        arrived(grad_in.at[0], pair_recv.at[9])
 
         @pl.loop(0, blocks)
         def _(k):
-            block = grad_in[:, pl.ds(k, 1)].astype(F32).reshape(n * cap, 2 * width).astype(BF16)
+            block = jnp.concatenate([grad_in[core, :, pl.ds(k, 1)].astype(F32) for core in range(CORES)], axis=1)
+            block = block.reshape(n * cap, 2 * width).astype(BF16)
             both_halves = lax.dot_general(block, pick(k), (((0,), (0,)), ((), ())), preferred_element_type=F32)
             low = lax.broadcasted_iota(jnp.int32, (width, LANES), 1) < seg
             grads = jnp.where(low, both_halves[0:width], both_halves[width : 2 * width])
@@ -385,54 +413,60 @@
     product(1)
     hop(1, 1)
     hop(0, 2)
-    for d in ((1, 2), (3, 2)):
-        got(1, d)
-        relay("x", 1, d)
-        e = (d[1], d[0])
-        got(0, e)
-        relay("y", 0, e)
+    lend(0)
+    exit_and_rank_gradients()
+    got(1, (1, 2))
+    relay("x", 1, (1, 2))
+    got(0, (2, 1))
+    relay("y", 0, (2, 1))
     hop(0, 3)
+    got(1, (3, 2))
+    relay("x", 1, (3, 2))
+    got(0, (2, 3))
+    relay("y", 0, (2, 3))
     hop(1, 2)
-    exit_and_rank_gradients()
+    lend(1)
     for part in (0, 1):
         for d in ((2, 0), (0, 2), (1, 2)):
             if (part, d) not in ((0, (2, 0)), (1, (0, 2)), (1, (1, 2))):
                 got(part, d)
     product(2)
     hop(2, 1)
-    hop(1, 3)
-    hop(0, 4)
     for part in (0, 1):
         for d in ((2, 1), (2, 3), (3, 2), (2, 2)):
             if (part, d) not in ((0, (2, 1)), (0, (2, 3)), (1, (3, 2))):
                 got(part, d)
     product(3)
     hop(3, 1)
+    hop(1, 3)
+    hop(0, 4)
+    issued = len(sent)
+    lend(2)
+    lend(3)
+    swap_gradients()
     hop(2, 2)
+    spread_gradients()
+    hop(3, 2)
     hop(1, 4)
     finish(0)
-    spread_gradients()
-    hop(3, 2)
+    entry_gradient(0)
     hop(2, 3)
+    entry_gradient(1)
     finish(1)
-    entry_gradient(0)
-    entry_gradient(1)
     hop(3, 3)
+    entry_gradient(2)
     hop(2, 4)
-    entry_gradient(2)
     entry_gradient(3)
+    drain(issued)
     hop(3, 4)
-    close(0)
-    close(1)
     finish(2)
-    close(2)
     finish(3)
-    close(3)
 
     for copy in sent:
         copy.wait_send()
-    for k, src in enumerate((rank_in, sens_in, grad_in)):
-        arrived(src.at[pl.ds(0, n - 1)], all_send.at[k])
+    arrived(rank_in.at[pl.ds(0, RING - 1)], all_send.at[0])
+    arrived(sens_in.at[pl.ds(0, n - 1)], all_send.at[1])
+    arrived(rank_in.at[pl.ds(0, RING - 1)], all_send.at[2])
 
 
 def on_device(x, w, e, b, sens, user_ids, slot_table, counts):
@@ -453,9 +487,9 @@
     out, exit_grad, entry_grad = pl.pallas_call(
         exchange,
         out_shape=(
-            jax.ShapeDtypeStruct((tok, features), BF16),
-            jax.ShapeDtypeStruct((width, features), F32),
-            jax.ShapeDtypeStruct((adapters * width, depth), F32),
+            pltpu.VMEM((tok, features), BF16),
+            pltpu.VMEM((width, features), F32),
+            pltpu.VMEM((adapters * width, depth), F32),
         ),
         in_specs=[pl.BlockSpec(memory_space=pl.ANY)] * 5 + [vmem] + [smem] * 2,
         out_specs=(vmem,) * 3,
@@ -468,38 +502,43 @@
             pltpu.VMEM((blocks, LANES), jnp.int32),
             pltpu.VMEM((blocks, LANES), F32),
             pltpu.VMEM((blocks, LANES), F32),
-            pltpu.VMEM((n, blocks, cap, 2 * width), BF16),
+            pltpu.VMEM((CORES, RING, blocks, cap, 2 * width), BF16),
             pltpu.VMEM((n, cap, features), BF16),
             pltpu.VMEM((rows, depth), BF16),
             pltpu.VMEM((2, GROUPS, depth, wide), BF16),
             pltpu.VMEM((width, features), BF16),
             pltpu.VMEM((GROUPS, 2 * width, wide), BF16),
             pltpu.VMEM((GROUPS, rows, wide), F32),
-            pltpu.VMEM((n, blocks, cap, 2 * width), BF16),
+            pltpu.VMEM((RING, blocks, cap, 2 * width), BF16),
+            pltpu.VMEM((RING, blocks, cap, 2 * width), BF16),
+            pltpu.VMEM((RING, blocks, cap, 2 * width), BF16),
             pltpu.VMEM((slots // 2, 2 * width), F32),
             pltpu.VMEM((slots // 2, 2 * width), F32),
             pltpu.VMEM((rows, 2 * width), BF16),
             pltpu.VMEM((n, cap, features), BF16),
             pltpu.VMEM((blocks, cap, 2 * width), BF16),
-            pltpu.VMEM((n, blocks, cap, 2 * width), BF16),
+            pltpu.VMEM((CORES, RING, blocks, cap, 2 * width), BF16),
             pltpu.VMEM((adapters * width, rows), BF16),
             pltpu.VMEM((hops, chip_rows, wide), BF16),
             pltpu.VMEM((hops, chip_rows, wide), BF16),
             pltpu.VMEM((GROUPS, tok, wide), BF16),
             pltpu.VMEM((GROUPS, tok, wide), BF16),
+            pltpu.VMEM((GROUPS, 2, CORES, tok, wide), BF16),
             pltpu.VMEM((slots, width), F32),
             pltpu.SemaphoreType.DMA((40,)),
             pltpu.SemaphoreType.DMA((40,)),
             pltpu.SemaphoreType.DMA((hops,)),
             pltpu.SemaphoreType.DMA((hops,)),
-            pltpu.SemaphoreType.DMA((8,)),
-            pltpu.SemaphoreType.DMA((8,)),
+            pltpu.SemaphoreType.DMA((10,)),
+            pltpu.SemaphoreType.DMA((10,)),
             pltpu.SemaphoreType.DMA((3,)),
             pltpu.SemaphoreType.DMA((3,)),
             pltpu.SemaphoreType.DMA((5,)),
+            pltpu.SemaphoreType.DMA((4 * GROUPS,)),
+            pltpu.SemaphoreType.DMA((4 * GROUPS,)),
         ],
         compiler_params=pltpu.CompilerParams(
-            collective_id=0, has_side_effects=True, vmem_limit_bytes=62 * 1024 * 1024
+            collective_id=0, has_side_effects=True, vmem_limit_bytes=54 * 1024 * 1024
         ),
     )(
         x,

time: 103 us -> 89.2 us (0.87)
  Pallas kernels: 94.7 us -> 84.8 us
  local copies, waits for them, and re-layouts: 7.17 us -> 3.6 us
    pallas_call x1, Pallas kernels: 94.7 us -> 84.8 us  [on_device(): pl.pallas_call(exchange, out_shape=(pltpu.VMEM((tok, features), BF16), pl...]
    unnamed x5 -> x3, local copies, waits for them, and re-layouts: 7.17 us -> 3.6 us
where the time goes in v3:
time: 89.2 us; the launch traced here: 89.1 us
  Pallas kernels  84.8 us (95%)
  local copies, waits for them, and re-layouts  3.6 us (4%)
    pallas_call x1, Pallas kernels, on_device(): pl.pallas_call(exchange, out_shape=(pltpu.VMEM((tok, features), BF16), pl...  84.8 us
    unnamed x3, local copies, waits for them, and re-layouts  3.6 us

profile of v3, /device:TPU:1, one launch (start us, length us, event | category | flops | bytes accessed | tf_op | source)
XLA Modules:
  0.0 89.1 jit_solution(16105249303617530298)
XLA Ops:
  0.6 84.8 %shard_map.103 = (bf16[64,4096]{1,0:T(8,128)(2,1)S(1)}, f32[64,4096]{1,0:T(8,128)S(1)}, f32[1024,896]{1,0:T(8,128)S(1)}) custom-call(bf16[1024,896]{1,0:T(8,128)(2,1)} %bitcast.21, bf16[896,256]{1,0:T(8,128)(2,1)} %w_in.1, bf16[64,4096]{1,0:T(8,128)(2,1)} %bitcast.23, bf16[1024,896]{1,0:T(8,128)(2,1)} %bitcast.22, bf16[64,4096]{1,0:T(8,128)(2,1)} %bitcast.24, ...), custom_call_target="tpu_custom_call" | custom-call | tf_op jit(solution)/shard_map/pallas_call | solution.py:487
  85.4 0.8 copy.14
  86.2 1.8 %copy.15 = f32[1,16,896,64]{2,3,1,0:T(8,128)} copy(f32[1,16,896,64]{2,3,1,0:T(8,128)S(1)} %bitcast.18) | data formatting | bytes 7340032
  88.1 1.0 %copy.16 = f32[1,1,64,4096]{3,2,1,0:T(8,128)} copy(f32[1,1,64,4096]{3,2,1,0:T(8,128)S(1)} %bitcast.19) | data formatting | bytes 2097152

commit v4 on v3

--- a/solution.py
+++ b/solution.py
@@ -23,19 +23,13 @@
 LANES = 128
 
 
-def halved(part, offset):
-    dx, dy = offset
-    first, last = (dx, dy) if part == 0 else (dy, dx)
-    return last == 2 or (last == 0 and first == 2)
-
-
 def exchange(
-    x_in, w_in, b_in, e_in, cotangent, users_ref, table_ref, counts_ref,
+    x_in, w_in, b_in, e_in, cotangent, users_in, table_in, counts_in,
     out_ref, exit_ref, entry_ref,
-    x_ref, w_ref, b_ref, e_ref, sens_ref, owner_ref, slot_ref, column_ref, ranks_out, sens_out,
+    x_ref, w_ref, b_ref, e_ref, sens_ref, users_ref, table_ref, counts_ref, owner_ref, slot_ref, column_ref, ranks_out, sens_out,
     x_sib, w_all, b_sib, b_all, y_all, rank_pair, pair_sum, rank_in, rank_own, rank_sib, rank_rows, sens_in, grad_out, grad_in, grad_rows,
-    part_out, part_in, near_out, near_in, last_in, grad_sum,
-    ag_send, ag_recv, rs_send, rs_recv, pair_send, pair_recv, all_send, all_recv, load, last_send, last_recv,
+    part_out, part_in, near_out, last_in, grad_sum,
+    ag_send, ag_recv, rs_send, rs_recv, pair_send, pair_recv, all_send, all_recv, load, last_recv,
 ):
     n = RING * CORES
     dp = lax.axis_index("dp")
@@ -61,7 +55,10 @@
     loads = [
         pltpu.make_async_copy(src, dst, load.at[k])
         for k, (src, dst) in enumerate(
-            ((cotangent, sens_ref), (w_in, w_ref), (x_in, x_ref), (b_in, b_ref), (e_in, e_ref))
+            (
+                (users_in, users_ref), (table_in, table_ref), (counts_in, counts_ref), (cotangent, sens_ref),
+                (w_in, w_ref), (x_in, x_ref), (b_in, b_ref), (e_in, e_ref),
+            )
         )
     ]
     for copy in loads:
@@ -77,6 +74,8 @@
     seg = rows // n
     cap = seg // 8
     blocks = rows // LANES
+    for copy in loads[0:3]:
+        copy.wait()
     users = users_ref[...]
     line = lax.broadcasted_iota(jnp.int32, users.shape, 0)
     lane = lax.broadcasted_iota(jnp.int32, users.shape, 1)
@@ -106,43 +105,38 @@
     def pick(k):
         return jnp.where(slot_ref[pl.ds(k, 1), :] == slot_ids, 1.0, 0.0).astype(BF16)
 
-    loads[0].wait()
+    loads[3].wait()
     one_hot = jnp.where((slot_ref[pl.ds(z, 1), :] == slot_ids) & (in_upper == (c == 1)), 1.0, 0.0).astype(BF16)
 
-    @pl.loop(0, features // wide)
-    def _(i):
-        at = pl.ds(pl.multiple_of(i * wide, wide), wide)
-        block = sens_ref[:, at]
+    for i in range(features // wide):
+        block = sens_ref[:, i * wide : (i + 1) * wide]
         chosen = jnp.dot(one_hot, jnp.concatenate([block, block], axis=0), preferred_element_type=F32)
-        sens_out[:, :, at] = chosen.reshape(n, cap, wide).astype(BF16)
-
-    for copy in loads[1:4]:
-        copy.wait()
+        sens_out[:, :, i * wide : (i + 1) * wide] = chosen.reshape(n, cap, wide).astype(BF16)
     pl.semaphore_wait(barrier, n - 1 + 4)
 
-    sent = []
+    waits = []
 
     def send(src, dst, send_sem, recv_sem, to):
         copy = pltpu.make_async_remote_copy(
             src_ref=src, dst_ref=dst, send_sem=send_sem, recv_sem=recv_sem, device_id=to, device_id_type=MESH
         )
         copy.start()
-        sent.append(copy)
+        return copy
 
     def arrived(dst, sem):
         pltpu.make_async_copy(dst, dst, sem).wait()
 
     names = {}
 
-    def sem_of(part, offset, piece):
-        return names.setdefault((part, offset, piece), len(names))
+    def sem_of(part, offset):
+        return names.setdefault((part, offset), len(names))
 
     def place(part, offset, piece=None):
         spot = ORDER.index(offset)
         cols = pl.ds(LANES * (spot % GROUPS), LANES)
         if piece is None:
-            return w_all.at[part, spot // GROUPS, :, cols]
-        return w_all.at[part, spot // GROUPS, pl.ds(half * piece, half), cols]
+            return w_all.at[part * GROUPS + spot // GROUPS, :, cols]
+        return w_all.at[part * GROUPS + spot // GROUPS, pl.ds(half * piece, half), cols]
 
     def pass_on(axis, sign, part, offset, piece=None, src=None):
         dx, dy = offset
@@ -150,12 +144,11 @@
         to = at_x(sign) if axis == "x" else at_y(sign)
         if src is None:
             src = place(part, offset, piece)
-        num = sem_of(part, seen, piece)
-        send(src, place(part, seen, piece), ag_send.at[num], ag_recv.at[num], {"mp": to})
+        send_sem = ag_send.at[0 if piece is None else 1]
+        send(src, place(part, seen, piece), send_sem, ag_recv.at[sem_of(part, seen)], {"mp": to})
 
     def got(part, offset):
-        for piece in (0, 1) if halved(part, offset) else (None,):
-            arrived(place(part, offset, piece), ag_recv.at[sem_of(part, offset, piece)])
+        arrived(place(part, offset), ag_recv.at[sem_of(part, offset)])
 
     def both(axis, part, offset, src=None):
         for sign in (1, -1):
@@ -190,21 +183,23 @@
         lax.fori_loop(1, RING, body, 0)
 
     to_all(1, lambda to: sens_out.at[to], sens_in, ((5, 7), (10, 12)))
+    for copy in loads[4:7]:
+        copy.wait()
 
     own_cols = w_ref.at[:, pl.ds(pl.multiple_of(LANES * c, LANES), LANES)]
     sib_cols = w_ref.at[:, pl.ds(pl.multiple_of(LANES * (1 - c), LANES), LANES)]
-    send(sib_cols, place(1, (0, 0)), pair_send.at[0], pair_recv.at[0], {"dp": sib})
+    waits.append(send(sib_cols, place(1, (0, 0)), pair_send.at[0], pair_recv.at[0], {"dp": sib}))
     both("x", 0, (0, 0), own_cols)
-    send(x_ref, x_sib, pair_send.at[1], pair_recv.at[1], {"dp": sib})
-    send(b_ref, b_sib, pair_send.at[2], pair_recv.at[2], {"dp": sib})
-    w_all[0, 0, :, 0:LANES] = own_cols[...]
+    waits.append(send(x_ref, x_sib, pair_send.at[1], pair_recv.at[1], {"dp": sib}))
+    waits.append(send(b_ref, b_sib, pair_send.at[2], pair_recv.at[2], {"dp": sib}))
+    w_all[0, :, 0:LANES] = own_cols[...]
     sens_in[dp] = sens_out[dp]
     arrived(place(1, (0, 0)), pair_recv.at[0])
     both("y", 1, (0, 0))
     both("y", 0, (0, 0), own_cols)
     both("x", 1, (0, 0))
 
-    loads[4].wait()
+    loads[7].wait()
 
     @pl.loop(0, blocks // 2)
     def _(i):
@@ -226,11 +221,11 @@
             for core in range(CORES):
                 ranks_out[core, :, pl.ds(2 * i + j, 1)] = placed[:, core]
 
-    send(ranks_out.at[1 - c], rank_pair, pair_send.at[8], pair_recv.at[8], {"dp": sib})
-    arrived(rank_pair, pair_recv.at[8])
+    waits.append(send(ranks_out.at[1 - c], rank_pair, pair_send.at[4], pair_recv.at[4], {"dp": sib}))
+    arrived(rank_pair, pair_recv.at[4])
     pair_sum[...] = (ranks_out[c].astype(F32) + rank_pair[...].astype(F32)).astype(BF16)
     to_chips(0, lambda to: pair_sum.at[to], rank_in.at[z])
-    to_all(1, lambda to: sens_out.at[to], sens_in, ((1, 5), (7, 10), (12, n)))
+    to_all(1, lambda to: sens_out.at[to], sens_in, ((1, 5), (7, 8), (12, n)))
     rank_in[z] = pair_sum[z]
 
     for d in ((1, 0), (3, 0)):
@@ -262,7 +257,7 @@
     for k in range(1, RING):
         total = total + rank_in[k].astype(F32)
     rank_own[...] = total.reshape(rank_own.shape)
-    send(rank_own, rank_sib, pair_send.at[3], pair_recv.at[3], {"dp": sib})
+    waits.append(send(rank_own, rank_sib, pair_send.at[3], pair_recv.at[3], {"dp": sib}))
     arrived(rank_sib, pair_recv.at[3])
     mine, theirs = rank_own[...], rank_sib[...]
     low = lax.broadcasted_iota(jnp.int32, mine.shape, 1) < width
@@ -293,8 +288,8 @@
         def _(i):
             at = pl.ds(pl.multiple_of(i * tile, tile), tile)
             y_all[g, at] = (
-                jnp.dot(x_ref[at], w_all[0, g], preferred_element_type=F32)
-                + jnp.dot(x_sib[at], w_all[1, g], preferred_element_type=F32)
+                jnp.dot(x_ref[at], w_all[g], preferred_element_type=F32)
+                + jnp.dot(x_sib[at], w_all[GROUPS + g], preferred_element_type=F32)
                 + jnp.dot(rank_rows[at], b_all[g], preferred_element_type=F32)
             )
 
@@ -315,13 +310,12 @@
             part_out[num] = value.astype(BF16)
             to = ((z + RING + way) % RING) * CORES
             if step < length:
-                send(part_out.at[num], part_in.at[num], rs_send.at[num], rs_recv.at[num], {"dp": to + c})
+                send(part_out.at[num], part_in.at[num], rs_send.at[0], rs_recv.at[num], {"dp": to + c})
                 continue
             side = (1 + way) // 2
             for core in range(CORES):
                 piece = part_out.at[num, pl.ds(core * own_rows, own_rows)]
-                out_sem = last_send.at[g * 4 + side * 2 + core]
-                send(piece, last_in.at[g, side, c], out_sem, last_recv.at[g * 4 + side * 2 + c], {"dp": to + core})
+                send(piece, last_in.at[g, side * CORES + c], rs_send.at[0], last_recv.at[g], {"dp": to + core})
 
     def store(value, g, core):
         for j in range(GROUPS):
@@ -335,22 +329,15 @@
 
     def lend(g):
         near_out[g] = rows_of(g, 1 - c).astype(BF16)
-        send(near_out.at[g], near_in.at[g], pair_send.at[4 + g], pair_recv.at[4 + g], {"dp": sib})
+        send(near_out.at[g], last_in.at[g, 2 * CORES], rs_send.at[1], last_recv.at[g], {"dp": sib})
 
     def finish(g):
-        arrived(near_in.at[g], pair_recv.at[4 + g])
-        for side in range(2):
-            for core in range(CORES):
-                arrived(last_in.at[g, side, core], last_recv.at[g * 4 + side * 2 + core])
-        value = rows_of(g, c) + last_in[g, 0, c].astype(F32) + last_in[g, 1, c].astype(F32)
+        arrived(last_in.at[g], last_recv.at[g])
+        value = rows_of(g, c) + last_in[g, c].astype(F32) + last_in[g, CORES + c].astype(F32)
         store(value.astype(BF16), g, c)
-        value = near_in[g].astype(F32) + last_in[g, 0, 1 - c].astype(F32) + last_in[g, 1, 1 - c].astype(F32)
+        value = last_in[g, 2 * CORES].astype(F32)
+        value = value + last_in[g, 1 - c].astype(F32) + last_in[g, CORES + 1 - c].astype(F32)
         store(value.astype(BF16), g, 1 - c)
-
-    def drain(count):
-        for copy in sent[:count]:
-            copy.wait_send()
-        del sent[:count]
 
     def exit_and_rank_gradients():
         arrived(sens_in.at[pl.ds(0, n - 1)], all_recv.at[1])
@@ -376,10 +363,10 @@
 
     def swap_gradients():
         arrived(grad_in.at[0, pl.ds(0, RING - 1)], all_recv.at[2])
-        send(grad_in.at[c], grad_in.at[c], pair_send.at[9], pair_recv.at[9], {"dp": sib})
+        waits.append(send(grad_in.at[c], grad_in.at[c], pair_send.at[5], pair_recv.at[5], {"dp": sib}))
 
     def spread_gradients():
-        arrived(grad_in.at[0], pair_recv.at[9])
+        arrived(grad_in.at[0], pair_recv.at[5])
 
         @pl.loop(0, blocks)
         def _(k):
@@ -398,34 +385,31 @@
         at = slice(i * tile, (i + 1) * tile)
         entry_ref[at] = jnp.dot(grad_rows[at], x_ref[...], preferred_element_type=F32)
 
-    product(0)
-    hop(0, 1)
-    for d in ((1, 1), (3, 1), (1, 3), (3, 3)):
+    def relay_both(d):
         got(1, d)
         relay("x", 1, d)
         e = (d[1], d[0])
         got(0, e)
         relay("y", 0, e)
+
+    product(0)
+    hop(0, 1)
+    to_all(1, lambda to: sens_out.at[to], sens_in, ((8, 10),))
+    for d in ((1, 1), (3, 1), (1, 3), (3, 3)):
+        relay_both(d)
+    hop(0, 2)
     got(0, (2, 0))
     both("y", 0, (2, 0))
     got(1, (0, 2))
     both("x", 1, (0, 2))
     product(1)
     hop(1, 1)
-    hop(0, 2)
     lend(0)
     exit_and_rank_gradients()
-    got(1, (1, 2))
-    relay("x", 1, (1, 2))
-    got(0, (2, 1))
-    relay("y", 0, (2, 1))
     hop(0, 3)
-    got(1, (3, 2))
-    relay("x", 1, (3, 2))
-    got(0, (2, 3))
-    relay("y", 0, (2, 3))
+    relay_both((1, 2))
     hop(1, 2)
-    lend(1)
+    relay_both((3, 2))
     for part in (0, 1):
         for d in ((2, 0), (0, 2), (1, 2)):
             if (part, d) not in ((0, (2, 0)), (1, (0, 2)), (1, (1, 2))):
@@ -438,35 +422,48 @@
                 got(part, d)
     product(3)
     hop(3, 1)
+    hop(0, 4)
     hop(1, 3)
-    hop(0, 4)
-    issued = len(sent)
+    lend(1)
     lend(2)
     lend(3)
+    hop(2, 2)
     swap_gradients()
-    hop(2, 2)
-    spread_gradients()
     hop(3, 2)
     hop(1, 4)
     finish(0)
+    hop(2, 3)
+    spread_gradients()
+    hop(3, 3)
+    finish(1)
     entry_gradient(0)
-    hop(2, 3)
     entry_gradient(1)
-    finish(1)
-    hop(3, 3)
+    hop(2, 4)
     entry_gradient(2)
-    hop(2, 4)
     entry_gradient(3)
-    drain(issued)
     hop(3, 4)
-    finish(2)
-    finish(3)
-
-    for copy in sent:
+    for copy in waits:
         copy.wait_send()
+    arrived(w_all.at[pl.ds(0, 5)], ag_send.at[0])
+    arrived(w_all.at[pl.ds(0, 5), pl.ds(0, half)], ag_send.at[1])
     arrived(rank_in.at[pl.ds(0, RING - 1)], all_send.at[0])
     arrived(sens_in.at[pl.ds(0, n - 1)], all_send.at[1])
     arrived(rank_in.at[pl.ds(0, RING - 1)], all_send.at[2])
+    arrived(near_out, rs_send.at[1])
+    finish(2)
+    finish(3)
+    arrived(part_out, rs_send.at[0])
+
+
+def store_results(out_vmem, exit_vmem, entry_vmem, out_ref, exit_ref, entry_ref, sem):
+    copies = [
+        pltpu.make_async_copy(src, dst, sem.at[k])
+        for k, (src, dst) in enumerate(((entry_vmem, entry_ref), (exit_vmem, exit_ref), (out_vmem, out_ref)))
+    ]
+    for copy in copies:
+        copy.start()
+    for copy in copies:
+        copy.wait()
 
 
 def on_device(x, w, e, b, sens, user_ids, slot_table, counts):
@@ -483,7 +480,6 @@
     hops = GROUPS * (RING - 1)
     chip_rows = rows // RING
     vmem = pl.BlockSpec(memory_space=pltpu.VMEM)
-    smem = pl.BlockSpec(memory_space=pltpu.SMEM)
     out, exit_grad, entry_grad = pl.pallas_call(
         exchange,
         out_shape=(
@@ -491,7 +487,7 @@
             pltpu.VMEM((width, features), F32),
             pltpu.VMEM((adapters * width, depth), F32),
         ),
-        in_specs=[pl.BlockSpec(memory_space=pl.ANY)] * 5 + [vmem] + [smem] * 2,
+        in_specs=[pl.BlockSpec(memory_space=pl.ANY)] * 8,
         out_specs=(vmem,) * 3,
         scratch_shapes=[
             pltpu.VMEM((rows, depth), BF16),
@@ -500,12 +496,15 @@
             pltpu.VMEM((adapters * width, depth), BF16),
             pltpu.VMEM((tok, features), BF16),
             pltpu.VMEM((blocks, LANES), jnp.int32),
+            pltpu.SMEM((adapters,), jnp.int32),
+            pltpu.SMEM((n,), jnp.int32),
+            pltpu.VMEM((blocks, LANES), jnp.int32),
             pltpu.VMEM((blocks, LANES), F32),
             pltpu.VMEM((blocks, LANES), F32),
             pltpu.VMEM((CORES, RING, blocks, cap, 2 * width), BF16),
             pltpu.VMEM((n, cap, features), BF16),
             pltpu.VMEM((rows, depth), BF16),
-            pltpu.VMEM((2, GROUPS, depth, wide), BF16),
+            pltpu.VMEM((2 * GROUPS, depth, wide), BF16),
             pltpu.VMEM((width, features), BF16),
             pltpu.VMEM((GROUPS, 2 * width, wide), BF16),
             pltpu.VMEM((GROUPS, rows, wide), F32),
@@ -522,20 +521,18 @@
             pltpu.VMEM((hops, chip_rows, wide), BF16),
             pltpu.VMEM((hops, chip_rows, wide), BF16),
             pltpu.VMEM((GROUPS, tok, wide), BF16),
-            pltpu.VMEM((GROUPS, tok, wide), BF16),
-            pltpu.VMEM((GROUPS, 2, CORES, tok, wide), BF16),
+            pltpu.VMEM((GROUPS, 2 * CORES + 1, tok, wide), BF16),
             pltpu.VMEM((slots, width), F32),
-            pltpu.SemaphoreType.DMA((40,)),
-            pltpu.SemaphoreType.DMA((40,)),
+            pltpu.SemaphoreType.DMA((2,)),
+            pltpu.SemaphoreType.DMA((2 * (len(ORDER) - 1),)),
+            pltpu.SemaphoreType.DMA((2,)),
             pltpu.SemaphoreType.DMA((hops,)),
-            pltpu.SemaphoreType.DMA((hops,)),
-            pltpu.SemaphoreType.DMA((10,)),
-            pltpu.SemaphoreType.DMA((10,)),
+            pltpu.SemaphoreType.DMA((6,)),
+            pltpu.SemaphoreType.DMA((6,)),
             pltpu.SemaphoreType.DMA((3,)),
             pltpu.SemaphoreType.DMA((3,)),
-            pltpu.SemaphoreType.DMA((5,)),
-            pltpu.SemaphoreType.DMA((4 * GROUPS,)),
-            pltpu.SemaphoreType.DMA((4 * GROUPS,)),
+            pltpu.SemaphoreType.DMA((8,)),
+            pltpu.SemaphoreType.DMA((GROUPS,)),
         ],
         compiler_params=pltpu.CompilerParams(
             collective_id=0, has_side_effects=True, vmem_limit_bytes=54 * 1024 * 1024
@@ -550,6 +547,15 @@
         slot_table[0],
         counts[0],
     )
+    anywhere = pl.BlockSpec(memory_space=pl.ANY)
+    out, exit_grad, entry_grad = pl.pallas_call(
+        store_results,
+        out_shape=[jax.ShapeDtypeStruct(a.shape, a.dtype) for a in (out, exit_grad, entry_grad)],
+        in_specs=[anywhere] * 3,
+        out_specs=[anywhere] * 3,
+        scratch_shapes=[pltpu.SemaphoreType.DMA((3,))],
+        compiler_params=pltpu.CompilerParams(vmem_limit_bytes=1024 * 1024),
+    )(out, exit_grad, entry_grad)
     entry_grad = entry_grad.reshape(adapters, width, depth).transpose(0, 2, 1)
     return out[None], entry_grad[None], exit_grad[None, None]
 

time: 89.2 us -> 86 us (0.964)
  local copies, waits for them, and re-layouts: 3.6 us -> 0 us
    unnamed x3 -> x0, local copies, waits for them, and re-layouts: 3.6 us -> none
    pallas_call x0 -> x1, Pallas kernels: none -> 2.37 us  [on_device(): pl.pallas_call(store_results, out_shape=[jax.ShapeDtypeStruct(a.shape, a....]
    pallas_call x1, Pallas kernels: 84.8 us -> 82.9 us  [on_device(): pl.pallas_call(exchange, out_shape=(pltpu.VMEM((tok, features), BF16), pl...]
where the time goes in v4:
time: 86 us; the launch traced here: 85.9 us
  Pallas kernels  85.2 us (99%)
    pallas_call x1, Pallas kernels, on_device(): pl.pallas_call(exchange, out_shape=(pltpu.VMEM((tok, features), BF16), pl...  82.9 us
    pallas_call x1, Pallas kernels, on_device(): pl.pallas_call(store_results, out_shape=[jax.ShapeDtypeStruct(a.shape, a....  2.37 us

profile of v4, /device:TPU:1, one launch (start us, length us, event | category | flops | bytes accessed | tf_op | source)
XLA Modules:
  0.0 85.9 jit_solution(16453467023743638900)
XLA Ops:
  0.6 82.9 %shard_map.103 = (bf16[64,4096]{1,0:T(8,128)(2,1)S(1)}, f32[64,4096]{1,0:T(8,128)S(1)}, f32[1024,896]{1,0:T(8,128)S(1)}) custom-call(bf16[1024,896]{1,0:T(8,128)(2,1)} %bitcast.18, bf16[896,256]{1,0:T(8,128)(2,1)} %w_in.1, bf16[64,4096]{1,0:T(8,128)(2,1)} %bitcast.20, bf16[1024,896]{1,0:T(8,128)(2,1)} %bitcast.19, bf16[64,4096]{1,0:T(8,128)(2,1)} %bitcast.21, ...), custom_call_target="tpu_custom_call" | custom-call | tf_op jit(solution)/shard_map/pallas_call | solution.py:483
  83.5 2.4 %shard_map.104 = (bf16[64,4096]{1,0:T(8,128)(2,1)}, f32[64,4096]{1,0:T(8,128)}, f32[1024,896]{1,0:T(8,128)}) custom-call(bf16[64,4096]{1,0:T(8,128)(2,1)S(1)} %get-tuple-element.9.out_vmem, f32[64,4096]{1,0:T(8,128)S(1)} %get-tuple-element.10.exit_vmem, f32[1024,896]{1,0:T(8,128)S(1)} %get-tuple-element.11.entry_vmem), custom_call_target="tpu_custom_call" | custom-call | tf_op jit(solution)/shard_map/pallas_call | solution.py:551

commit v5 on v4

--- a/solution.py
+++ b/solution.py
@@ -358,6 +358,8 @@
         grad = grad_sum[...].reshape(blocks, 2, cap, width)
         halves = [grad[:, k].reshape(blocks * cap, width) for k in range(2)]
         grad_out[...] = jnp.concatenate(halves, axis=1).reshape(blocks, cap, 2 * width).astype(BF16)
+
+    def send_gradients():
         to_chips(2, lambda to: grad_out, grad_in.at[c, z])
         grad_in[c, z] = grad_out[...]
 
@@ -409,6 +411,7 @@
     hop(0, 3)
     relay_both((1, 2))
     hop(1, 2)
+    send_gradients()
     relay_both((3, 2))
     for part in (0, 1):
         for d in ((2, 0), (0, 2), (1, 2)):
@@ -422,7 +425,6 @@
                 got(part, d)
     product(3)
     hop(3, 1)
-    hop(0, 4)
     hop(1, 3)
     lend(1)
     lend(2)
@@ -430,18 +432,19 @@
     hop(2, 2)
     swap_gradients()
     hop(3, 2)
+    hop(0, 4)
+    spread_gradients()
+    entry_gradient(0)
+    entry_gradient(1)
+    hop(2, 3)
+    hop(3, 3)
     hop(1, 4)
     finish(0)
-    hop(2, 3)
-    spread_gradients()
-    hop(3, 3)
-    finish(1)
-    entry_gradient(0)
-    entry_gradient(1)
     hop(2, 4)
+    hop(3, 4)
     entry_gradient(2)
     entry_gradient(3)
-    hop(3, 4)
+    finish(1)
     for copy in waits:
         copy.wait_send()
     arrived(w_all.at[pl.ds(0, 5)], ag_send.at[0])

time: 86 us -> 84.9 us (0.987)
  Pallas kernels: 85.2 us -> 84.2 us
    pallas_call x1, Pallas kernels: 82.9 us -> 81.8 us  [on_device(): pl.pallas_call(exchange, out_shape=(pltpu.VMEM((tok, features), BF16), pl...]
where the time goes in v5:
time: 84.9 us; the launch traced here: 84.8 us
  Pallas kernels  84.2 us (99%)
    pallas_call x1, Pallas kernels, on_device(): pl.pallas_call(exchange, out_shape=(pltpu.VMEM((tok, features), BF16), pl...  81.8 us
    pallas_call x1, Pallas kernels, on_device(): pl.pallas_call(store_results, out_shape=[jax.ShapeDtypeStruct(a.shape, a....  2.37 us

profile of v5, /device:TPU:1, one launch (start us, length us, event | category | flops | bytes accessed | tf_op | source)
XLA Modules:
  0.0 84.8 jit_solution(4578600543859307060)
XLA Ops:
  0.6 81.8 %shard_map.103 = (bf16[64,4096]{1,0:T(8,128)(2,1)S(1)}, f32[64,4096]{1,0:T(8,128)S(1)}, f32[1024,896]{1,0:T(8,128)S(1)}) custom-call(bf16[1024,896]{1,0:T(8,128)(2,1)} %bitcast.18, bf16[896,256]{1,0:T(8,128)(2,1)} %w_in.1, bf16[64,4096]{1,0:T(8,128)(2,1)} %bitcast.20, bf16[1024,896]{1,0:T(8,128)(2,1)} %bitcast.19, bf16[64,4096]{1,0:T(8,128)(2,1)} %bitcast.21, ...), custom_call_target="tpu_custom_call" | custom-call | tf_op jit(solution)/shard_map/pallas_call | solution.py:486
  82.5 2.4 %shard_map.104 = (bf16[64,4096]{1,0:T(8,128)(2,1)}, f32[64,4096]{1,0:T(8,128)}, f32[1024,896]{1,0:T(8,128)}) custom-call(bf16[64,4096]{1,0:T(8,128)(2,1)S(1)} %get-tuple-element.9.out_vmem, f32[64,4096]{1,0:T(8,128)S(1)} %get-tuple-element.10.exit_vmem, f32[1024,896]{1,0:T(8,128)S(1)} %get-tuple-element.11.entry_vmem), custom_call_target="tpu_custom_call" | custom-call | tf_op jit(solution)/shard_map/pallas_call | solution.py:554

commit v6 on v5

--- a/solution.py
+++ b/solution.py
@@ -225,7 +225,7 @@
     arrived(rank_pair, pair_recv.at[4])
     pair_sum[...] = (ranks_out[c].astype(F32) + rank_pair[...].astype(F32)).astype(BF16)
     to_chips(0, lambda to: pair_sum.at[to], rank_in.at[z])
-    to_all(1, lambda to: sens_out.at[to], sens_in, ((1, 5), (7, 8), (12, n)))
+    to_all(1, lambda to: sens_out.at[to], sens_in, ((1, 5), (7, 9), (12, n)))
     rank_in[z] = pair_sum[z]
 
     for d in ((1, 0), (3, 0)):
@@ -296,6 +296,9 @@
     def sem_rs(g, way, step):
         return g * (RING - 1) + (step - 1 if way > 0 else UP[g] + step - 1)
 
+    def landing(g, way, step):
+        return g * (RING - 3) + (step - 1 if way > 0 else UP[g] + step - 2)
+
     def hop(g, step):
         for way, length in ((-1, DOWN[g]), (1, UP[g])):
             if step > length:
@@ -303,14 +306,15 @@
             dest = (z + RING + way * (length + 1 - step)) % RING
             value = y_all[g, pl.ds(pl.multiple_of(dest * chip_rows, chip_rows), chip_rows)]
             if step > 1:
-                before = sem_rs(g, way, step - 1)
+                before = landing(g, way, step - 1)
                 arrived(part_in.at[before], rs_recv.at[before])
                 value = value + part_in[before].astype(F32)
             num = sem_rs(g, way, step)
             part_out[num] = value.astype(BF16)
             to = ((z + RING + way) % RING) * CORES
             if step < length:
-                send(part_out.at[num], part_in.at[num], rs_send.at[0], rs_recv.at[num], {"dp": to + c})
+                into = landing(g, way, step)
+                send(part_out.at[num], part_in.at[into], rs_send.at[0], rs_recv.at[into], {"dp": to + c})
                 continue
             side = (1 + way) // 2
             for core in range(CORES):
@@ -396,7 +400,7 @@
 
     product(0)
     hop(0, 1)
-    to_all(1, lambda to: sens_out.at[to], sens_in, ((8, 10),))
+    to_all(1, lambda to: sens_out.at[to], sens_in, ((9, 10),))
     for d in ((1, 1), (3, 1), (1, 3), (3, 3)):
         relay_both(d)
     hop(0, 2)
@@ -440,8 +444,8 @@
     hop(3, 3)
     hop(1, 4)
     finish(0)
+    hop(3, 4)
     hop(2, 4)
-    hop(3, 4)
     entry_gradient(2)
     entry_gradient(3)
     finish(1)
@@ -522,14 +526,14 @@
             pltpu.VMEM((CORES, RING, blocks, cap, 2 * width), BF16),
             pltpu.VMEM((adapters * width, rows), BF16),
             pltpu.VMEM((hops, chip_rows, wide), BF16),
-            pltpu.VMEM((hops, chip_rows, wide), BF16),
+            pltpu.VMEM((GROUPS * (RING - 3), chip_rows, wide), BF16),
             pltpu.VMEM((GROUPS, tok, wide), BF16),
             pltpu.VMEM((GROUPS, 2 * CORES + 1, tok, wide), BF16),
             pltpu.VMEM((slots, width), F32),
             pltpu.SemaphoreType.DMA((2,)),
             pltpu.SemaphoreType.DMA((2 * (len(ORDER) - 1),)),
             pltpu.SemaphoreType.DMA((2,)),
-            pltpu.SemaphoreType.DMA((hops,)),
+            pltpu.SemaphoreType.DMA((GROUPS * (RING - 3),)),
             pltpu.SemaphoreType.DMA((6,)),
             pltpu.SemaphoreType.DMA((6,)),
             pltpu.SemaphoreType.DMA((3,)),

time: 84.9 us -> 83.7 us (0.986)
  Pallas kernels: 84.2 us -> 83 us
    pallas_call x1, Pallas kernels: 81.8 us -> 80.6 us  [on_device(): pl.pallas_call(exchange, out_shape=(pltpu.VMEM((tok, features), BF16), pl...]
where the time goes in v6:
time: 83.7 us; the launch traced here: 83.6 us
  Pallas kernels  83 us (99%)
    pallas_call x1, Pallas kernels, on_device(): pl.pallas_call(exchange, out_shape=(pltpu.VMEM((tok, features), BF16), pl...  80.6 us
    pallas_call x1, Pallas kernels, on_device(): pl.pallas_call(store_results, out_shape=[jax.ShapeDtypeStruct(a.shape, a....  2.37 us

profile of v6, /device:TPU:1, one launch (start us, length us, event | category | flops | bytes accessed | tf_op | source)
XLA Modules:
  0.0 83.6 jit_solution(714453330229607840)
XLA Ops:
  0.6 80.6 %shard_map.103 = (bf16[64,4096]{1,0:T(8,128)(2,1)S(1)}, f32[64,4096]{1,0:T(8,128)S(1)}, f32[1024,896]{1,0:T(8,128)S(1)}) custom-call(bf16[1024,896]{1,0:T(8,128)(2,1)} %bitcast.18, bf16[896,256]{1,0:T(8,128)(2,1)} %w_in.1, bf16[64,4096]{1,0:T(8,128)(2,1)} %bitcast.20, bf16[1024,896]{1,0:T(8,128)(2,1)} %bitcast.19, bf16[64,4096]{1,0:T(8,128)(2,1)} %bitcast.21, ...), custom_call_target="tpu_custom_call" | custom-call | tf_op jit(solution)/shard_map/pallas_call | solution.py:490
  81.2 2.4 %shard_map.104 = (bf16[64,4096]{1,0:T(8,128)(2,1)}, f32[64,4096]{1,0:T(8,128)}, f32[1024,896]{1,0:T(8,128)}) custom-call(bf16[64,4096]{1,0:T(8,128)(2,1)S(1)} %get-tuple-element.9.out_vmem, f32[64,4096]{1,0:T(8,128)S(1)} %get-tuple-element.10.exit_vmem, f32[1024,896]{1,0:T(8,128)S(1)} %get-tuple-element.11.entry_vmem), custom_call_target="tpu_custom_call" | custom-call | tf_op jit(solution)/shard_map/pallas_call | solution.py:558

commit v7 on v6

--- a/solution.py
+++ b/solution.py
@@ -443,11 +443,11 @@
     hop(2, 3)
     hop(3, 3)
     hop(1, 4)
-    finish(0)
     hop(3, 4)
     hop(2, 4)
     entry_gradient(2)
     entry_gradient(3)
+    finish(0)
     finish(1)
     for copy in waits:
         copy.wait_send()

time: 83.7 us -> 83.7 us (level)
  no operation moved by 1% of the time
where the time goes in v7:
time: 83.7 us; the launch traced here: 83.6 us
  Pallas kernels  83 us (99%)
    pallas_call x1, Pallas kernels, on_device(): pl.pallas_call(exchange, out_shape=(pltpu.VMEM((tok, features), BF16), pl...  80.6 us
    pallas_call x1, Pallas kernels, on_device(): pl.pallas_call(store_results, out_shape=[jax.ShapeDtypeStruct(a.shape, a....  2.37 us

profile of v7, /device:TPU:1, one launch (start us, length us, event | category | flops | bytes accessed | tf_op | source)
XLA Modules:
  0.0 83.6 jit_solution(2143077055311717539)
XLA Ops:
  0.6 80.6 %shard_map.103 = (bf16[64,4096]{1,0:T(8,128)(2,1)S(1)}, f32[64,4096]{1,0:T(8,128)S(1)}, f32[1024,896]{1,0:T(8,128)S(1)}) custom-call(bf16[1024,896]{1,0:T(8,128)(2,1)} %bitcast.18, bf16[896,256]{1,0:T(8,128)(2,1)} %w_in.1, bf16[64,4096]{1,0:T(8,128)(2,1)} %bitcast.20, bf16[1024,896]{1,0:T(8,128)(2,1)} %bitcast.19, bf16[64,4096]{1,0:T(8,128)(2,1)} %bitcast.21, ...), custom_call_target="tpu_custom_call" | custom-call | tf_op jit(solution)/shard_map/pallas_call | solution.py:490
  81.2 2.4 %shard_map.104 = (bf16[64,4096]{1,0:T(8,128)(2,1)}, f32[64,4096]{1,0:T(8,128)}, f32[1024,896]{1,0:T(8,128)}) custom-call(bf16[64,4096]{1,0:T(8,128)(2,1)S(1)} %get-tuple-element.9.out_vmem, f32[64,4096]{1,0:T(8,128)S(1)} %get-tuple-element.10.exit_vmem, f32[1024,896]{1,0:T(8,128)S(1)} %get-tuple-element.11.entry_vmem), custom_call_target="tpu_custom_call" | custom-call | tf_op jit(solution)/shard_map/pallas_call | solution.py:558
